TPU v7x, 32 devices: a whole 2x2x4 slice. The times are simulated.
32 devices in a mesh: dp: 2 (over x), fsdp: 4 (over z), expert: 4 (over y, core).
Axes of the slice: x: 2, y: 2, z: 4, core: 2. Of those that a mesh axis runs over, the one named last changes fastest.
Arguments:
- window: bfloat16 [256, 4096], P('fsdp'), may hold values from -3 to 3
- attention_gain: float32 [4096], replicated, may hold values from 0.1 to 1.9
- query_weight: bfloat16 [4096, 4096], P('fsdp', 'expert'), may hold values from -0.09375 to 0.09375
- key_weight: bfloat16 [4096, 1024], P('fsdp', 'expert'), may hold values from -0.1875 to 0.1875
- value_weight: bfloat16 [4096, 1024], P('fsdp', 'expert'), may hold values from -0.1875 to 0.1875
- out_weight: bfloat16 [4096, 4096], P('expert', 'fsdp'), may hold values from -0.1875 to 0.1875
- cache_keys: bfloat16 [1024, 1024], P('dp', 'expert'), may hold values from -104 to 104
- cache_values: bfloat16 [1024, 1024], P('dp', 'expert'), may hold values from -12 to 12
- occluded: int32 [1024, 2], P('dp'), may hold values from 0 to 1, as said below
- feedforward_gain: float32 [4096], replicated, may hold values from 0.1 to 1.9
- router_weight: bfloat16 [4096, 4], replicated, may hold values from -0.0234375 to 0.0234375
- chosen_experts: int32 [2, 256, 2], P('dp', 'fsdp'), may hold values from 0 to 3, all different within a row; in each aligned block of 64 rows (0 to 63, 64 to 127, ..., all dimensions but the last counted through in order) at most 64 rows name the same one
- gate_weight: bfloat16 [4, 12288, 4096], P('expert', ('dp', 'fsdp')), may hold values from -0.09375 to 0.09375
- up_weight: bfloat16 [4, 12288, 4096], P('expert', ('dp', 'fsdp')), may hold values from -0.09375 to 0.09375
- down_weight: bfloat16 [4, 12288, 4096], P('expert', ('dp', 'fsdp')), may hold values from -0.0546875 to 0.0546875
Outputs:
- layer_output: bfloat16 [2, 256, 4096], P('dp', 'fsdp')
Inputs may be any that keep to these rules, and one draw needn't show every extreme that they name: `chosen_experts`: each row names 2 different experts. In each aligned block of 64 rows, counting the leading dimensions together (the rows of one device), no expert is named by more than 64 rows, a bound that some block reaches. `occluded`: constant over each aligned run of 64 prefix positions.
All inputs are finite; a program needn't handle non-finite values.
Results may differ from a plain program's by a relative error of at most 0.0095.
The roundings to bfloat16 on the way count: a program that leaves them out, or rounds other values in their place, can miss the bound.
Values may be sent and summed in bfloat16 or wider, within the bound.
A program may use at most 128 MiB of HBM per device.

v0:
```python
import jax
import jax.numpy as jnp
from jax import lax
from jax.sharding import PartitionSpec as P

HD = 128
TOP = 2


epsilon = 1e-05
rope_base = 1000000.0
floor_score = -1e30


def rms_norm(values, scales):
    widened = values.astype(jnp.float32)
    inverse = lax.rsqrt(jnp.mean(widened * widened, axis=-1, keepdims=True) + epsilon)
    return (widened * inverse * scales).astype(jnp.bfloat16)


def rotate(vectors, positions):
    halfway = vectors.shape[-1] // 2
    powers = jnp.arange(halfway, dtype=jnp.float32) * (2.0 / vectors.shape[-1])
    frequency = rope_base ** (-powers)
    angles = positions.astype(jnp.float32)[:, None] * frequency[None, :]
    cosine = jnp.cos(angles)[:, None, :]
    sine_part = jnp.sin(angles)[:, None, :]
    former = vectors[..., :halfway]
    latter = vectors[..., halfway:]
    return jnp.concatenate(
        [former * cosine - latter * sine_part, latter * cosine + former * sine_part], axis=-1
    )


def absorb_block(running, scores, visible, values_block):
    running_top, running_total, running_output = running
    masked = jnp.where(visible, scores, floor_score)
    fresh_top = jnp.maximum(running_top, jnp.max(masked, axis=-1))
    weights = jnp.where(visible, jnp.exp(masked - fresh_top[..., None]), 0.0)
    fresh_total = jnp.sum(weights, axis=-1)
    fresh_output = jnp.einsum(
        "kgtn,nkd->kgtd",
        weights.astype(jnp.bfloat16),
        values_block,
        preferred_element_type=jnp.float32,
    )
    return (fresh_top, fresh_total, fresh_output)


def local(
    window,
    attention_gain,
    query_weight,
    key_weight,
    value_weight,
    out_weight,
    cache_keys,
    cache_values,
    occluded,
    feedforward_gain,
    router_weight,
    chosen_experts,
    gate_weight,
    up_weight,
    down_weight,
):
    token_rows = window.shape[0]
    fsdp_count = lax.axis_size("fsdp")
    fsdp_place = lax.axis_index("fsdp")
    data_place = lax.axis_index("dp")
    expert_place = lax.axis_index("expert")
    query_heads = query_weight.shape[1] // HD
    key_heads = key_weight.shape[1] // HD
    grouping = query_heads // key_heads
    window_rows = token_rows * fsdp_count
    prefix_rows = cache_keys.shape[0] * lax.axis_size("dp")
    score_scale = HD ** (-0.5)
    normed = rms_norm(window, attention_gain)
    first_row = fsdp_place * token_rows
    own_positions = prefix_rows + first_row + jnp.arange(token_rows, dtype=jnp.int32)
    all_positions = prefix_rows + jnp.arange(window_rows, dtype=jnp.int32)
    everyone = lax.all_gather(normed, "fsdp", axis=0, tiled=True)
    slab_width = query_weight.shape[0]
    columns = lax.dynamic_slice_in_dim(everyone, fsdp_place * slab_width, slab_width, 1)
    row_block = columns
    query_sum = lax.psum_scatter(
        jnp.dot(row_block, query_weight, preferred_element_type=jnp.float32),
        "fsdp",
        scatter_dimension=0,
        tiled=True,
    )
    key_sum, value_sum = lax.psum(
        (
            jnp.dot(columns, key_weight, preferred_element_type=jnp.float32),
            jnp.dot(columns, value_weight, preferred_element_type=jnp.float32),
        ),
        "fsdp",
    )
    queries = rotate(query_sum.reshape(token_rows, query_heads, HD), own_positions).astype(
        jnp.bfloat16
    )
    window_keys = (
        rotate(key_sum.reshape(window_rows, key_heads, HD), all_positions)
        .astype(jnp.bfloat16)
        .reshape(window_rows, key_heads * HD)
    )
    window_values = value_sum.astype(jnp.bfloat16)
    query_grid = queries.reshape(token_rows, key_heads, grouping, HD)
    fresh_keys = window_keys.reshape(window_rows, key_heads, HD)
    fresh_values = window_values.reshape(window_rows, key_heads, HD)
    window_scores = (
        jnp.einsum("tkgd,nkd->kgtn", query_grid, fresh_keys, preferred_element_type=jnp.float32)
        * score_scale
    )
    causal = jnp.arange(window_rows)[None, :] <= (first_row + jnp.arange(token_rows))[:, None]
    empty_state = (
        jnp.full((key_heads, grouping, token_rows), floor_score, jnp.float32),
        jnp.zeros((key_heads, grouping, token_rows), jnp.float32),
        jnp.zeros((key_heads, grouping, token_rows, HD), jnp.float32),
    )
    window_state = absorb_block(empty_state, window_scores, causal, fresh_values)
    occluded_flags = occluded.astype(jnp.bfloat16)
    keys_block = lax.all_gather(cache_keys, "dp", axis=0, tiled=True)
    values_block = lax.all_gather(cache_values, "dp", axis=0, tiled=True)
    flags_block = lax.all_gather(occluded_flags, "dp", axis=0, tiled=True)
    block_length = keys_block.shape[0]
    scores = (
        jnp.einsum(
            "tkgd,nkd->kgtn",
            query_grid,
            keys_block.reshape(block_length, key_heads, HD),
            preferred_element_type=jnp.float32,
        )
        * score_scale
    )
    visible = lax.dynamic_slice_in_dim(flags_block, data_place, 1, 1)[:, 0] == 0
    prefix_state = absorb_block(
        empty_state, scores, visible, values_block.reshape(block_length, key_heads, HD)
    )
    overall = jnp.maximum(prefix_state[0], window_state[0])
    prefix_fade = jnp.exp(prefix_state[0] - overall)
    window_fade = jnp.exp(window_state[0] - overall)
    denominator = prefix_state[1] * prefix_fade + window_state[1] * window_fade
    head_values = (
        prefix_state[2] * prefix_fade[..., None] + window_state[2] * window_fade[..., None]
    ) / denominator[..., None]
    attended = (
        head_values.transpose(2, 0, 1, 3).reshape(token_rows, query_heads * HD).astype(jnp.bfloat16)
    )
    head_terms = jnp.dot(
        attended,
        lax.all_gather(out_weight, "fsdp", axis=1, tiled=True),
        preferred_element_type=jnp.float32,
    )
    residual = window.astype(jnp.float32) + lax.psum(head_terms, "expert")
    normed_mix = rms_norm(residual, feedforward_gain)
    logits = jnp.dot(normed_mix, router_weight, preferred_element_type=jnp.float32)
    expert_count = router_weight.shape[1]
    expert_picks = chosen_experts.reshape(token_rows, TOP)
    matches = expert_picks[:, :, None] == jnp.arange(expert_count, dtype=jnp.int32)[None, None, :]
    picked = jnp.sum(jnp.where(matches, logits[:, None, :], 0.0), axis=-1)
    gate_shares = jax.nn.sigmoid(picked - picked[:, ::-1])
    expert_hits = expert_picks == expert_place
    taken_flag = jnp.any(expert_hits, axis=1).astype(jnp.int32)
    weight_mine = jnp.sum(jnp.where(expert_hits, gate_shares, 0.0), axis=1)
    capacity = min(token_rows, 2 * token_rows * TOP // expert_count)
    slot_numbers = jnp.cumsum(taken_flag) - taken_flag
    placing = (slot_numbers[:, None] == jnp.arange(capacity, dtype=jnp.int32)[None, :]) & (
        taken_flag[:, None] == 1
    )
    send_rows = lax.dot_general(
        placing.astype(jnp.bfloat16),
        normed_mix,
        (((0,), (0,)), ((), ())),
        preferred_element_type=jnp.float32,
    ).astype(jnp.bfloat16)
    gate_rows = gate_weight[0]
    up_rows = up_weight[0]
    down_rows = down_weight[0]
    contract_last = (((1,), (1,)), ((), ()))
    piece_rows = lax.all_gather(send_rows, ("dp", "fsdp"), axis=0, tiled=True)
    gate_values = lax.dot_general(
        piece_rows, gate_rows, contract_last, preferred_element_type=jnp.float32
    )
    lifted = lax.dot_general(piece_rows, up_rows, contract_last, preferred_element_type=jnp.float32)
    hidden = (jax.nn.silu(gate_values) * lifted).astype(jnp.bfloat16)
    row_block = hidden
    expert_output = lax.psum_scatter(
        jnp.dot(row_block, down_rows, preferred_element_type=jnp.float32).astype(jnp.bfloat16),
        ("dp", "fsdp"),
        scatter_dimension=0,
        tiled=True,
    ).astype(jnp.float32)
    returned = jnp.dot(
        placing.astype(jnp.float32),
        expert_output,
        precision=lax.Precision.HIGHEST,
        preferred_element_type=jnp.float32,
    )
    mixture = lax.psum(returned * weight_mine[:, None], "expert")
    return (residual + mixture).astype(jnp.bfloat16).reshape(1, token_rows, residual.shape[1])


def solution(mesh):
    placed = (
        P("fsdp", None),
        P(),
        P("fsdp", "expert"),
        P("fsdp", "expert"),
        P("fsdp", "expert"),
        P("expert", "fsdp"),
        P("dp", "expert"),
        P("dp", "expert"),
        P("dp", None),
        P(),
        P(),
        P("dp", "fsdp", None),
        P("expert", ("dp", "fsdp"), None),
        P("expert", ("dp", "fsdp"), None),
        P("expert", ("dp", "fsdp"), None),
    )
    return jax.shard_map(
        local, mesh=mesh, in_specs=placed, out_specs=P("dp", "fsdp", None), check_vma=False
    )
```

profile of v0, /device:TPU:0, one launch (start us, length us, event | category | flops | bytes accessed | tf_op | source)
XLA Modules:
  0.0 560.7 jit_solution(14526967308801473713)
XLA Ops:
  6.5 1.4 fusion.29
  8.0 2.0 fusion.31
  10.1 48.7 %all-gather.4.cloned.1.call-done = bf16[256,4096]{1,0:T(8,128)(2,1)} async-done(((bf16[64,4096]{1,0:T(8,128)(2,1)}), bf16[256,4096]{1,0:T(8,128)(2,1)}) %all-gather.4.cloned.1.call-update) | async-done | bytes 2097168 | tf_op jit(solution)/shard_map/all_gather | solution.py:82
  58.8 1.4 fusion.43
  60.2 0.8 copy.41
  61.1 2.7 fusion.45
  63.9 0.5 all-gather.6.cloned.1.call-update
  65.1 4.3 all_gather.18
  69.5 7.9 %all_gather.20 = bf16[1024,256]{0,1:T(8,128)(2,1)S(1)} all-gather(bf16[512,256]{0,1:T(8,128)(2,1)S(1)} %copy.37), channel_id=1, replica_groups=mesh['dp'=2,'fsdp'=4,'expert'=4] {'dp'}, dimensions={0}, use_global_device_ids=true | all-gather | bytes 786432 | tf_op jit(solution)/shard_map/all_gather | solution.py:123
  77.4 7.1 %all_gather.21 = bf16[1024,256]{0,1:T(8,128)(2,1)S(1)} all-gather(bf16[512,256]{0,1:T(8,128)(2,1)S(1)} %copy.39), channel_id=1, replica_groups=mesh['dp'=2,'fsdp'=4,'expert'=4] {'dp'}, dimensions={0}, use_global_device_ids=true | all-gather | bytes 786432 | tf_op jit(solution)/shard_map/all_gather | solution.py:124
  84.8 0.5 multiply_cosine_fusion
  85.3 1.3 fusion.41
  86.7 23.1 %all-reduce.10 = bf16[256,256]{1,0:T(8,128)(2,1)S(1)} all-reduce(f32[256,256]{1,0:T(8,128)S(1)} %fusion.41), channel_id=1, replica_groups=mesh['dp'=2,'fsdp'=4,'expert'=4] {'fsdp'}, use_global_device_ids=true, to_apply=%region_5.6 | all-reduce | flops 65536 | bytes 393216 | tf_op jit(solution)/shard_map/psum | solution.py:92
  109.9 1.2 subtract_convert_fusion
  111.1 14.3 %reduce-scatter.3.cloned.1.call-done = f32[64,1024]{1,0:T(8,128)} async-done(((f32[256,1024]{1,0:T(8,128)}), f32[64,1024]{1,0:T(8,128)}) %reduce-scatter.3.cloned.1.call-update) | async-done | bytes 262160 | tf_op jit(solution)/shard_map/reduce_scatter | solution.py:86
  125.4 1.0 copy.55
  127.3 0.6 bitcast_reduce_fusion
  127.9 0.6 fusion.20
  128.6 0.6 fusion.27
  129.8 145.4 %all-gather.6.cloned.1.call-done = bf16[1024,4096]{1,0:T(8,128)(2,1)} async-done(((bf16[1024,1024]{1,0:T(8,128)(2,1)}), bf16[1024,4096]{1,0:T(8,128)(2,1)}) %all-gather.6.cloned.1.call-update) | async-done | bytes 8388624 | tf_op jit(solution)/shard_map/all_gather | solution.py:152
  275.1 6.0 %fusion.80 = f32[64,4096]{1,0:T(8,128)} fusion(bf16[64,1024]{1,0:T(8,128)(2,1)S(1)} %convert_element_type.96, bf16[1024,4096]{1,0:T(8,128)(2,1)} %all-gather.6.cloned.1.call-done), kind=kOutput, calls=%fused_computation.113 | convolution fusion | flops 536870912 | bytes 9568256 | tf_op jit(solution)/shard_map/dot_general | solution.py:150
  281.6 34.0 %all-reduce.7.cloned.1.call-done = f32[64,4096]{1,0:T(8,128)} async-done(((f32[64,4096]{1,0:T(8,128)}), f32[64,4096]{1,0:T(8,128)}) %all-reduce.7.cloned.1.call-update) | async-done | bytes 1048592 | tf_op jit(solution)/shard_map/psum | solution.py:155
  315.6 1.6 multiply_reduce_fusion
  317.4 1.2 convolution_convert_fusion
  318.9 73.7 %all-gather.8.cloned.1.call-done = bf16[512,4096]{1,0:T(8,128)(2,1)} async-done(((bf16[64,4096]{1,0:T(8,128)(2,1)}), bf16[512,4096]{1,0:T(8,128)(2,1)}) %all-gather.8.cloned.1.call-update) | async-done | bytes 4194320 | tf_op jit(solution)/shard_map/all_gather | solution.py:181
  392.6 12.1 %fusion.4 = f32[512,1536]{1,0:T(8,128)} fusion(bf16[512,4096]{1,0:T(8,128)(2,1)} %all-gather.8.cloned.1.call-done, bf16[1,1536,4096]{2,1,0:T(8,128)(2,1)} %param.27), kind=kOutput, calls=%fused_computation.4 | convolution fusion | flops 6442450944 | bytes 19922944 | tf_op jit(solution)/shard_map/dot_general | solution.py:182
  404.7 21.8 %fusion.6 = bf16[512,4096]{1,0:T(8,128)(2,1)} fusion(bf16[1,1536,4096]{2,1,0:T(8,128)(2,1)} %param.29, bf16[512,4096]{1,0:T(8,128)(2,1)} %all-gather.8.cloned.1.call-done, bf16[1,1536,4096]{2,1,0:T(8,128)(2,1)} %param.28, f32[512,1536]{1,0:T(8,128)} %fusion.4), kind=kOutput, calls=%fused_computation.6 | convolution fusion | flops 12891717632 | bytes 36700160 | tf_op jit(solution)/shard_map/dot_general | solution.py:189
  426.6 0.7 copy-done.8
  427.6 85.3 %reduce-scatter.5.cloned.1.call-done = bf16[64,4096]{1,0:T(8,128)(2,1)} async-done(((bf16[512,4096]{1,0:T(8,128)(2,1)}), bf16[64,4096]{1,0:T(8,128)(2,1)}) %reduce-scatter.5.cloned.1.call-update) | async-done | bytes 524304 | tf_op jit(solution)/shard_map/reduce_scatter | solution.py:188
  512.9 2.4 convolution_multiply_fusion
  515.4 36.0 %all-reduce.9.cloned.1.call-done = f32[64,4096]{1,0:T(8,128)} async-done(((f32[64,4096]{1,0:T(8,128)}), f32[64,4096]{1,0:T(8,128)}) %all-reduce.9.cloned.1.call-update) | async-done | bytes 1048592 | tf_op jit(solution)/shard_map/psum | solution.py:200
  551.3 2.5 fusion.38
  (74 shorter events, 3.8 us)
Async XLA Ops:
  6.5 54.6 %copy-start = (bf16[1024,1024]{1,0:T(8,128)(2,1)S(1)}, bf16[1024,1024]{1,0:T(8,128)(2,1)}, u32[]{:S(2)}) copy-start(bf16[1024,1024]{1,0:T(8,128)(2,1)} %param.17) | copy-start | bytes 6291460
  6.5 52.3 %copy-start.4 = (bf16[1024,256]{1,0:T(8,128)(2,1)S(1)}, bf16[1024,256]{1,0:T(8,128)(2,1)}, u32[]{:S(2)}) copy-start(bf16[1024,256]{1,0:T(8,128)(2,1)} %param.18) | copy-start | bytes 1572868
  6.5 52.3 %all-gather.4.cloned.1.call-start = ((), (), s32[]{:S(2)}) async-start(), calls=%async_computation.2 | async-start | bytes 2621440 | tf_op jit(solution)/shard_map/all_gather | solution.py:82
  10.0 99.9 %all-reduce.5.cloned.1.call-start = ((), (), s32[]{:S(2)}) async-start(), calls=%async_computation.4 | async-start | bytes 524288 | tf_op jit(solution)/shard_map/psum | solution.py:92
  61.1 64.4 %reduce-scatter.3.cloned.1.call-start = ((), (), s32[]{:S(2)}) async-start(), calls=%async_computation.3 | async-start | bytes 1310720 | tf_op jit(solution)/shard_map/reduce_scatter | solution.py:86
  63.9 0.7 copy-start.11
  63.9 1.0 copy-start.6
  63.9 1.1 copy-start.7
  63.9 21.4 %copy-start.5 = (bf16[1024,256]{1,0:T(8,128)(2,1)S(1)}, bf16[1024,256]{1,0:T(8,128)(2,1)}, u32[]{:S(2)}) copy-start(bf16[1024,256]{1,0:T(8,128)(2,1)} %param.19) | copy-start | bytes 1572868
  63.9 211.2 %all-gather.6.cloned.1.call-start = ((), (), s32[]{:S(2)}) async-start(), calls=%async_computation.5 | async-start | bytes 10485760 | tf_op jit(solution)/shard_map/all_gather | solution.py:152
  64.5 251.1 %all-reduce.7.cloned.1.call-start = ((), (), s32[]{:S(2)}) async-start(), calls=%async_computation.6 | async-start | bytes 2097152 | tf_op jit(solution)/shard_map/psum | solution.py:155
  129.7 151.5 %copy-start.10 = (s32[1,64,2]{1,2,0:T(2,128)S(1)}, s32[1,64,2]{1,2,0:T(2,128)}, u32[]{:S(2)}) copy-start(s32[1,64,2]{1,2,0:T(2,128)} %param.26) | copy-start | bytes 1540
  129.7 185.9 %copy-start.2 = (bf16[64,4096]{1,0:T(8,128)(2,1)S(1)}, bf16[64,4096]{1,0:T(8,128)(2,1)}, u32[]{:S(2)}) copy-start(bf16[64,4096]{1,0:T(8,128)(2,1)} %param.15) | copy-start | bytes 1572868
  281.2 36.0 %copy-start.9 = (f32[4096]{0:T(1024)S(1)}, f32[4096]{0:T(1024)}, u32[]{:S(2)}) copy-start(f32[4096]{0:T(1024)} %param.24) | copy-start | bytes 49156
  281.2 111.4 %all-gather.8.cloned.1.call-start = ((), (), s32[]{:S(2)}) async-start(), calls=%async_computation.7 | async-start | bytes 4718592 | tf_op jit(solution)/shard_map/all_gather | solution.py:181
  315.6 1.6 copy-start.3
  318.7 194.2 %reduce-scatter.5.cloned.1.call-start = ((), (), s32[]{:S(2)}) async-start(), calls=%async_computation.8 | async-start | bytes 4718592 | tf_op jit(solution)/shard_map/reduce_scatter | solution.py:188
  426.5 0.8 copy-start.8
  426.5 124.8 %all-reduce.9.cloned.1.call-start = ((), (), s32[]{:S(2)}) async-start(), calls=%async_computation.9 | async-start | bytes 2097152 | tf_op jit(solution)/shard_map/psum | solution.py:200
  515.3 38.5 %copy-start.1 = (bf16[1024,1024]{1,0:T(8,128)(2,1)S(1)}, bf16[1024,1024]{1,0:T(8,128)(2,1)}, u32[]{:S(2)}) copy-start(bf16[1024,1024]{1,0:T(8,128)(2,1)} %param.17) | copy-start | bytes 6291460
Sparse Core Ops, SparseCore 0:
  10.1 48.6 all-gather.3
  61.2 34.6 all-reduce.4
  98.2 27.1 reduce-scatter.2
  126.8 148.2 all-gather.5
  281.3 34.2 all-reduce.6
  318.8 73.7 all-gather.7
  426.7 86.1 reduce-scatter.4
  515.5 35.8 all-reduce.8
where the time goes:
time: 561 us
  waiting for transfers between devices  438 us (78%)
  matrix products  51.2 us (9%)
  blocking collectives  42.4 us (8%)
  between operations  13.8 us (2%)
  other arithmetic  11.1 us (2%)
    all_gather x1, waiting for transfers between devices, local(): lax.all_gather(out_weight, 'fsdp', axis=1, tiled=True)  145 us
    reduce_scatter x1, waiting for transfers between devices, local(): lax.psum_scatter(jnp.dot(row_block, down_rows, preferred_element_type=jnp...  85.3 us
    all_gather x1, waiting for transfers between devices, local(): piece_rows = lax.all_gather(send_rows, ('dp', 'fsdp'), axis=0, tiled=True)  73.7 us
    all_gather x1, waiting for transfers between devices, local(): everyone = lax.all_gather(normed, 'fsdp', axis=0, tiled=True)  48.7 us
    psum x1, waiting for transfers between devices, local(): mixture = lax.psum(returned * weight_mine[:, None], 'expert')  36 us
    psum x1, waiting for transfers between devices, local(): residual = window.astype(jnp.float32) + lax.psum(head_terms, 'expert')  34 us
    psum x1, blocking collectives, local(): lax.psum((jnp.dot(columns, key_weight, preferred_element_type=jnp.float32...  23.1 us
    dot_general x1, matrix products, local(): jnp.dot(row_block, down_rows, preferred_element_type=jnp.float32)  21.8 us
  transfers between devices with their start and end apart: 8, of which 7 were waited for; matrix products, arithmetic and copies ran while one was open for 2% of the time, Pallas kernels for 0%

commit v1 on v0

v1 whole, which is shorter than its diff:
```python
import functools

import jax
import jax.numpy as jnp
from jax import lax
from jax.experimental import pallas as pl
from jax.experimental.pallas import tpu as pltpu
from jax.sharding import PartitionSpec as P

HD = 128
TOP = 2

epsilon = 1e-05
rope_base = 1000000.0
floor_score = -1e30
MESH = pl.DeviceIdType.MESH


def rms_norm(values, scales):
    widened = values.astype(jnp.float32)
    inverse = lax.rsqrt(jnp.mean(widened * widened, axis=-1, keepdims=True) + epsilon)
    return (widened * inverse * scales).astype(jnp.bfloat16)


def rotate(vectors, positions):
    halfway = vectors.shape[-1] // 2
    powers = jnp.arange(halfway, dtype=jnp.float32) * (2.0 / vectors.shape[-1])
    frequency = rope_base ** (-powers)
    angles = positions.astype(jnp.float32)[:, None] * frequency[None, :]
    cosine = jnp.cos(angles)[:, None, :]
    sine_part = jnp.sin(angles)[:, None, :]
    former = vectors[..., :halfway]
    latter = vectors[..., halfway:]
    return jnp.concatenate(
        [former * cosine - latter * sine_part, latter * cosine + former * sine_part], axis=-1
    )


def linear_place(axes, sizes):
    place = 0
    for axis in axes:
        place = place * sizes[axis] + lax.axis_index(axis)
    return place


def coordinates(axes, sizes, place):
    found = {}
    for axis in reversed(axes):
        found[axis] = lax.rem(place, sizes[axis])
        place = place // sizes[axis]
    return found


def count(axes, sizes):
    total = 1
    for axis in axes:
        total *= sizes[axis]
    return total


def source_part(kind, ref, to):
    if kind == "gather":
        return ref
    if kind == "rows":
        return ref.at[to]
    if kind == "second":
        return ref.at[:, to]
    if kind == "rows_to_columns":
        return ref.at[to]
    raise ValueError(kind)


def exchange_kernel(kinds, sizes, *refs):
    n = len(kinds)
    inputs, outputs, sems = refs[:n], refs[n : 2 * n], refs[2 * n :]
    barrier = pltpu.get_barrier_semaphore()
    total = 0
    for _, axes in kinds:
        size = count(axes, sizes)
        here = linear_place(axes, sizes)
        for k in range(1, size):
            to = coordinates(axes, sizes, lax.rem(here + k, size))
            pl.semaphore_signal(barrier, inc=1, device_id=to, device_id_type=MESH)
        total += size - 1
    local_copies = []

    def landing(kind, out, here, width):
        if kind == "rows_to_columns":
            return out.at[:, pl.ds(pl.multiple_of(here * width, 128), width)]
        return out.at[here]

    def part(kind, ref, to, size):
        if kind == "columns":
            width = ref.shape[1] // size
            return ref.at[:, pl.ds(pl.multiple_of(to * width, 128), width)]
        return source_part(kind, ref, to)

    for i, (kind, axes) in enumerate(kinds):
        size = count(axes, sizes)
        here = linear_place(axes, sizes)
        width = inputs[i].shape[-1]
        own = pltpu.make_async_copy(
            part(kind, inputs[i], here, size),
            landing(kind, outputs[i], here, width),
            sems[3 * i + 2].at[0],
        )
        own.start()
        local_copies.append(own)
    pl.semaphore_wait(barrier, total)
    copies = []
    for i, (kind, axes) in enumerate(kinds):
        size = count(axes, sizes)
        here = linear_place(axes, sizes)
        width = inputs[i].shape[-1]
        for k in range(1, size):
            place = lax.rem(here + k, size)
            copy = pltpu.make_async_remote_copy(
                src_ref=part(kind, inputs[i], place, size),
                dst_ref=landing(kind, outputs[i], here, width),
                send_sem=sems[3 * i].at[k - 1],
                recv_sem=sems[3 * i + 1].at[k - 1],
                device_id=coordinates(axes, sizes, place),
                device_id_type=MESH,
            )
            copy.start()
            copies.append(copy)
    for own in local_copies:
        own.wait()
    for copy in copies:
        copy.wait()


def exchange(sizes, number, *items):
    kinds = tuple((kind, axes) for _, kind, axes in items)
    shapes, scratch = [], []
    for array, kind, axes in items:
        size = count(axes, sizes)
        if kind == "gather":
            shape = (size,) + array.shape
        elif kind == "rows":
            shape = array.shape
        elif kind == "second":
            shape = (size, array.shape[0]) + array.shape[2:]
        elif kind == "columns":
            shape = (size, array.shape[0], array.shape[1] // size)
        else:
            shape = (array.shape[1], size * array.shape[2])
        shapes.append(jax.ShapeDtypeStruct(shape, array.dtype))
        scratch += [
            pltpu.SemaphoreType.DMA((size - 1,)),
            pltpu.SemaphoreType.DMA((size - 1,)),
            pltpu.SemaphoreType.DMA((1,)),
        ]
    return pl.pallas_call(
        functools.partial(exchange_kernel, kinds, sizes),
        out_shape=tuple(shapes),
        in_specs=[pl.BlockSpec(memory_space=pl.ANY)] * len(items),
        out_specs=tuple(pl.BlockSpec(memory_space=pl.ANY) for _ in items),
        scratch_shapes=scratch,
        compiler_params=pltpu.CompilerParams(collective_id=number, has_side_effects=True),
        name=f"exchange_{number}",
    )(*(array for array, _, _ in items))


def greet(sizes):
    d, f, e = lax.axis_index("dp"), lax.axis_index("fsdp"), lax.axis_index("expert")
    levels = sizes["expert"] // 2
    y, c = e // 2, lax.rem(e, 2)
    barrier = pltpu.get_barrier_semaphore()
    others = []
    for k in range(1, sizes["dp"]):
        others.append({"dp": lax.rem(d + k, sizes["dp"])})
    for k in range(1, sizes["fsdp"]):
        others.append({"fsdp": lax.rem(f + k, sizes["fsdp"])})
    for k in range(1, levels):
        others.append({"expert": lax.rem(y + k, levels) * 2 + c})
    others.append({"expert": y * 2 + 1 - c})
    for other in others:
        pl.semaphore_signal(barrier, inc=1, device_id=other, device_id_type=MESH)
    pl.semaphore_wait(barrier, len(others))
    return d, f, e, y, c


class Sender:
    def __init__(self, send, recv):
        self.send, self.recv, self.next = send, recv, 0

    def __call__(self, source, target, device):
        copy = pltpu.make_async_remote_copy(
            src_ref=source,
            dst_ref=target,
            send_sem=self.send.at[self.next],
            recv_sem=self.recv.at[self.next],
            device_id=device,
            device_id_type=MESH,
        )
        self.next += 1
        copy.start()
        return copy


def spread_kernel(sizes, x_ref, g_ref, out, gates, send, recv, local):
    dps, fs, levels = sizes["dp"], sizes["fsdp"], sizes["expert"] // 2
    own = [
        pltpu.make_async_copy(
            x_ref,
            out.at[
                lax.axis_index("dp"),
                lax.axis_index("fsdp"),
                lax.axis_index("expert") // 2,
                lax.rem(lax.axis_index("expert"), 2),
            ],
            local.at[0],
        ),
        pltpu.make_async_copy(
            g_ref,
            gates.at[
                lax.axis_index("dp"),
                lax.axis_index("fsdp"),
                lax.axis_index("expert") // 2,
                lax.rem(lax.axis_index("expert"), 2),
            ],
            local.at[1],
        ),
    ]
    for copy in own:
        copy.start()
    d, f, e, y, c = greet(sizes)
    half = x_ref.shape[-1] // 2
    low, high = pl.ds(0, half), pl.ds(half, half)
    go = Sender(send, recv)
    copies = []
    for k in range(1, fs):
        to = {"fsdp": lax.rem(f + k, fs)}
        copies.append(go(x_ref, out.at[d, f, y, c], to))
        copies.append(go(g_ref, gates.at[d, f, y, c], to))
    for copy in own:
        copy.wait()
    for copy in copies:
        copy.wait()
    copies = []
    for k in range(1, dps):
        to = {"dp": lax.rem(d + k, dps)}
        part = out.at[d, :, y, c, :, low]
        copies.append(go(part, part, to))
        part = gates.at[d, :, y, c]
        copies.append(go(part, part, to))
    for k in range(1, levels):
        to = {"expert": lax.rem(y + k, levels) * 2 + c}
        part = out.at[d, :, y, c, :, high]
        copies.append(go(part, part, to))
    for copy in copies:
        copy.wait()
    copies = []
    for k in range(1, levels):
        to = {"expert": lax.rem(y + k, levels) * 2 + c}
        part = out.at[:, :, y, c, :, low]
        copies.append(go(part, part, to))
        part = gates.at[:, :, y, c]
        copies.append(go(part, part, to))
    for k in range(1, dps):
        to = {"dp": lax.rem(d + k, dps)}
        part = out.at[d, :, :, c, :, high]
        copies.append(go(part, part, to))
    for copy in copies:
        copy.wait()
    to = {"expert": y * 2 + 1 - c}
    part = out.at[:, :, :, c]
    copies = [go(part, part, to)]
    part = gates.at[:, :, :, c]
    copies.append(go(part, part, to))
    for copy in copies:
        copy.wait()


def spread(sizes, number, rows, shares):
    dps, fs, levels = sizes["dp"], sizes["fsdp"], sizes["expert"] // 2
    lead = (dps, fs, levels, 2)
    sems = 2 * (fs - 1) + 3 * (dps - 1) + 3 * (levels - 1) + 2
    return pl.pallas_call(
        functools.partial(spread_kernel, sizes),
        out_shape=(
            jax.ShapeDtypeStruct(lead + rows.shape, rows.dtype),
            jax.ShapeDtypeStruct(lead + shares.shape, shares.dtype),
        ),
        in_specs=[pl.BlockSpec(memory_space=pl.ANY)] * 2,
        out_specs=(pl.BlockSpec(memory_space=pl.ANY),) * 2,
        scratch_shapes=[
            pltpu.SemaphoreType.DMA((sems,)),
            pltpu.SemaphoreType.DMA((sems,)),
            pltpu.SemaphoreType.DMA((2,)),
        ],
        compiler_params=pltpu.CompilerParams(collective_id=number, has_side_effects=True),
        name="spread",
    )(rows, shares)


def collect_kernel(
    sizes, x_ref, out, first, one, two_a, two_b, three, r1, r2a, r2b, r3a, r3b, r4, send, recv, local
):
    dps, fs, levels = sizes["dp"], sizes["fsdp"], sizes["expert"] // 2
    half = out.shape[-1] // 2
    low, high = pl.ds(0, half), pl.ds(half, half)
    own = pltpu.make_async_copy(
        x_ref.at[:, :, :, lax.rem(lax.axis_index("expert"), 2)], first, local.at[0]
    )
    own.start()
    d, f, e, y, c = greet(sizes)
    go = Sender(send, recv)
    copy = go(x_ref.at[:, :, :, 1 - c], r1, {"expert": y * 2 + 1 - c})
    own.wait()
    copy.wait()

    @pl.loop(0, dps * fs * levels)
    def _(i):
        p, q, r = i // (fs * levels), lax.rem(i // levels, fs), lax.rem(i, levels)
        one[p, q, r] = (
            first[p, q, r].astype(jnp.float32) + r1[p, q, r].astype(jnp.float32)
        ).astype(one.dtype)

    copies = []
    for k in range(1, dps):
        to = lax.rem(d + k, dps)
        copies.append(go(one.at[to, :, :, :, low], r2a.at[k - 1], {"dp": to}))
    for k in range(1, levels):
        to = lax.rem(y + k, levels)
        copies.append(go(one.at[:, :, to, :, high], r2b.at[k - 1], {"expert": to * 2 + c}))
    for copy in copies:
        copy.wait()

    @pl.loop(0, fs * levels)
    def _(i):
        q, r = i // levels, lax.rem(i, levels)
        total = one[d, q, r, :, low].astype(jnp.float32)
        for k in range(dps - 1):
            total += r2a[k, q, r].astype(jnp.float32)
        two_a[q, r] = total.astype(two_a.dtype)

    @pl.loop(0, dps * fs)
    def _(i):
        p, q = i // fs, lax.rem(i, fs)
        total = one[p, q, y, :, high].astype(jnp.float32)
        for k in range(levels - 1):
            total += r2b[k, p, q].astype(jnp.float32)
        two_b[p, q] = total.astype(two_b.dtype)

    copies = []
    for k in range(1, levels):
        to = lax.rem(y + k, levels)
        copies.append(go(two_a.at[:, to], r3a.at[k - 1], {"expert": to * 2 + c}))
    for k in range(1, dps):
        to = lax.rem(d + k, dps)
        copies.append(go(two_b.at[to], r3b.at[k - 1], {"dp": to}))
    for copy in copies:
        copy.wait()

    @pl.loop(0, fs)
    def _(q):
        total = two_a[q, y].astype(jnp.float32)
        for k in range(levels - 1):
            total += r3a[k, q].astype(jnp.float32)
        three[q, :, low] = total.astype(three.dtype)
        total = two_b[d, q].astype(jnp.float32)
        for k in range(dps - 1):
            total += r3b[k, q].astype(jnp.float32)
        three[q, :, high] = total.astype(three.dtype)

    copies = []
    for k in range(1, fs):
        to = lax.rem(f + k, fs)
        copies.append(go(three.at[to], r4.at[k - 1], {"fsdp": to}))
    for copy in copies:
        copy.wait()
    total = three[f].astype(jnp.float32)
    for k in range(fs - 1):
        total += r4[k].astype(jnp.float32)
    out[...] = total


def collect(sizes, number, terms):
    dps, fs, levels = sizes["dp"], sizes["fsdp"], sizes["expert"] // 2
    rows, width = terms.shape[-2:]
    half = width // 2
    kind = terms.dtype
    sems = 1 + 2 * (dps - 1) + 2 * (levels - 1) + (fs - 1)
    return pl.pallas_call(
        functools.partial(collect_kernel, sizes),
        out_shape=jax.ShapeDtypeStruct((rows, width), jnp.float32),
        in_specs=[pl.BlockSpec(memory_space=pl.ANY)],
        out_specs=pl.BlockSpec(memory_space=pltpu.VMEM),
        scratch_shapes=[
            pltpu.VMEM((dps, fs, levels, rows, width), kind),
            pltpu.VMEM((dps, fs, levels, rows, width), kind),
            pltpu.VMEM((fs, levels, rows, half), kind),
            pltpu.VMEM((dps, fs, rows, half), kind),
            pltpu.VMEM((fs, rows, width), kind),
            pltpu.VMEM((dps, fs, levels, rows, width), kind),
            pltpu.VMEM((dps - 1, fs, levels, rows, half), kind),
            pltpu.VMEM((levels - 1, dps, fs, rows, half), kind),
            pltpu.VMEM((levels - 1, fs, rows, half), kind),
            pltpu.VMEM((dps - 1, fs, rows, half), kind),
            pltpu.VMEM((fs - 1, rows, width), kind),
            pltpu.SemaphoreType.DMA((sems,)),
            pltpu.SemaphoreType.DMA((sems,)),
            pltpu.SemaphoreType.DMA((1,)),
        ],
        compiler_params=pltpu.CompilerParams(
            collective_id=number, has_side_effects=True, vmem_limit_bytes=56 << 20
        ),
        name="collect",
    )(terms)


def local(
    sizes,
    window,
    attention_gain,
    query_weight,
    key_weight,
    value_weight,
    out_weight,
    cache_keys,
    cache_values,
    occluded,
    feedforward_gain,
    router_weight,
    chosen_experts,
    gate_weight,
    up_weight,
    down_weight,
):
    dps, fs, es = sizes["dp"], sizes["fsdp"], sizes["expert"]
    token_rows, width = window.shape
    d, f, e = lax.axis_index("dp"), lax.axis_index("fsdp"), lax.axis_index("expert")
    query_width = query_weight.shape[1]
    key_width = key_weight.shape[1]
    query_heads = query_width // HD
    key_heads = key_width // HD
    grouping = query_heads // key_heads
    window_rows = token_rows * fs
    prefix_rows = cache_keys.shape[0] * dps
    score_scale = HD ** (-0.5)
    part = token_rows // dps
    sub = token_rows // es

    own_rows = lax.dynamic_slice_in_dim(window, d * part, part, 0)
    normed = rms_norm(own_rows, attention_gain)
    flags = occluded.astype(jnp.float32).T
    columns, keys_block, values_block, flags_block = exchange(
        sizes,
        0,
        (normed, "columns", ("fsdp",)),
        (cache_keys, "gather", ("dp",)),
        (cache_values, "gather", ("dp",)),
        (flags, "gather", ("dp",)),
    )
    columns = columns.reshape(fs * part, width // fs)
    sums = jnp.concatenate(
        [
            jnp.dot(columns, weight, preferred_element_type=jnp.float32)
            for weight in (query_weight, key_weight, value_weight)
        ],
        axis=1,
    )
    (sums,) = exchange(sizes, 1, (sums.reshape(fs, part, -1), "rows", ("fsdp",)))
    sums = jnp.sum(sums, axis=0)
    positions = prefix_rows + f * token_rows + d * part + jnp.arange(part, dtype=jnp.int32)
    rotated = rotate(
        sums[:, : query_width + key_width].reshape(part, query_heads + key_heads, HD), positions
    ).astype(jnp.bfloat16)
    queries = rotated[:, :query_heads].reshape(part, query_width)
    fresh = jnp.concatenate(
        [
            rotated[:, query_heads:].reshape(part, key_width),
            sums[:, query_width + key_width :].astype(jnp.bfloat16),
        ],
        axis=1,
    )
    queries, fresh = exchange(
        sizes, 2, (queries, "gather", ("dp",)), (fresh, "gather", ("fsdp", "dp"))
    )
    fresh = fresh.reshape(window_rows, 2 * key_width)
    query_grid = queries.reshape(token_rows, key_heads, grouping, HD)
    all_keys = jnp.concatenate(
        [keys_block.reshape(prefix_rows, key_width), fresh[:, :key_width]], axis=0
    ).reshape(prefix_rows + window_rows, key_heads, HD)
    all_values = jnp.concatenate(
        [values_block.reshape(prefix_rows, key_width), fresh[:, key_width:]], axis=0
    ).reshape(prefix_rows + window_rows, key_heads, HD)
    scores = (
        jnp.einsum("tkgd,nkd->kgtn", query_grid, all_keys, preferred_element_type=jnp.float32)
        * score_scale
    )
    seen = lax.dynamic_slice_in_dim(flags_block, d, 1, 1).reshape(prefix_rows) == 0
    causal = (
        jnp.arange(window_rows)[None, :]
        <= (f * token_rows + jnp.arange(token_rows))[:, None]
    )
    visible = jnp.concatenate(
        [jnp.broadcast_to(seen[None, :], (token_rows, prefix_rows)), causal], axis=1
    )
    masked = jnp.where(visible, scores, floor_score)
    top = jnp.max(masked, axis=-1, keepdims=True)
    weights = jnp.exp(masked - top)
    totals = jnp.sum(weights, axis=-1)
    heads = jnp.einsum(
        "kgtn,nkd->tkgd",
        weights.astype(jnp.bfloat16),
        all_values,
        preferred_element_type=jnp.float32,
    ) / totals.transpose(2, 0, 1)[..., None]
    attended = heads.reshape(token_rows, query_width).astype(jnp.bfloat16)

    (attended,) = exchange(sizes, 3, (attended, "gather", ("fsdp",)))
    head_terms = jnp.dot(
        attended.reshape(window_rows, query_width), out_weight, preferred_element_type=jnp.float32
    )
    (head_terms,) = exchange(
        sizes, 4, (head_terms.reshape(fs, es, sub, -1), "second", ("expert",))
    )
    (projected,) = exchange(
        sizes, 5, (jnp.sum(head_terms, axis=0), "rows_to_columns", ("fsdp",))
    )
    residual = lax.dynamic_slice_in_dim(window, e * sub, sub, 0).astype(jnp.float32) + projected
    normed_mix = rms_norm(residual, feedforward_gain)
    logits = jnp.dot(normed_mix, router_weight, preferred_element_type=jnp.float32)
    picks = lax.dynamic_slice_in_dim(chosen_experts.reshape(token_rows, TOP), e * sub, sub, 0)
    experts = router_weight.shape[1]
    matches = picks[:, :, None] == jnp.arange(experts, dtype=jnp.int32)[None, None, :]
    picked = jnp.sum(jnp.where(matches, logits[:, None, :], 0.0), axis=-1)
    gate_shares = jax.nn.sigmoid(picked - picked[:, ::-1])
    lanes = picks[:, :, None] == jnp.arange(128, dtype=jnp.int32)[None, None, :]
    shares = jnp.sum(jnp.where(lanes, gate_shares[:, :, None], 0.0), axis=1)

    rows, shares = spread(sizes, 6, normed_mix, shares)
    every = dps * window_rows
    rows = rows.reshape(every, width)
    share = lax.dynamic_slice_in_dim(shares.reshape(every, 128), e, 1, 1)
    contract_last = (((1,), (1,)), ((), ()))
    gate_values = lax.dot_general(
        rows, gate_weight[0], contract_last, preferred_element_type=jnp.float32
    )
    lifted = lax.dot_general(rows, up_weight[0], contract_last, preferred_element_type=jnp.float32)
    hidden = (jax.nn.silu(gate_values) * lifted).astype(jnp.bfloat16)
    terms = (
        jnp.dot(hidden, down_weight[0], preferred_element_type=jnp.float32) * share
    ).astype(jnp.bfloat16)
    mixture = collect(sizes, 7, terms.reshape(dps, fs, es // 2, 2, sub, width))
    (whole,) = exchange(
        sizes, 8, ((residual + mixture).astype(jnp.bfloat16), "gather", ("expert",))
    )
    return whole.reshape(1, token_rows, width)


def solution(mesh):
    sizes = dict(mesh.shape)
    placed = (
        P("fsdp", None),
        P(),
        P("fsdp", "expert"),
        P("fsdp", "expert"),
        P("fsdp", "expert"),
        P("expert", "fsdp"),
        P("dp", "expert"),
        P("dp", "expert"),
        P("dp", None),
        P(),
        P(),
        P("dp", "fsdp", None),
        P("expert", ("dp", "fsdp"), None),
        P("expert", ("dp", "fsdp"), None),
        P("expert", ("dp", "fsdp"), None),
    )
    return jax.shard_map(
        functools.partial(local, sizes),
        mesh=mesh,
        in_specs=placed,
        out_specs=P("dp", "fsdp", None),
        check_vma=False,
    )
```

time: 561 us -> 250 us (0.45)
  waiting for transfers between devices: 438 us -> 0 us
  Pallas kernels: 0 us -> 178 us
  blocking collectives: 42.4 us -> 0 us
  between operations: 13.8 us -> 0.33 us
  matrix products: 51.2 us -> 43.7 us
  local copies, waits for them, and re-layouts: 3.5 us -> 10.1 us
    all_gather x3 -> x0, waiting for transfers between devices: 268 us -> none  [the longest x1 145 us: local(): lax.all_gather(out_weight, 'fsdp', axis=1, tiled=True)]
    pallas_call x0 -> x9, Pallas kernels: none -> 178 us  [the longest x7 94.7 us: exchange(): pl.pallas_call(functools.partial(exchange_kernel, kinds, sizes), out_shap...]
    reduce_scatter x2 -> x0, waiting for transfers between devices: 99.6 us -> none  [the longest x1 85.3 us: local(): lax.psum_scatter(jnp.dot(row_block, down_rows, preferred_element_type=jnp...]
    psum x3 -> x0, waiting for transfers between devices: 70 us -> none  [the longest x1 36 us: local(): mixture = lax.psum(returned * weight_mine[:, None], 'expert')]
    psum x1 -> x0, blocking collectives: 23.1 us -> none  [local(): lax.psum((jnp.dot(columns, key_weight, preferred_element_type=jnp.float32...]
    all_gather x3 -> x0, blocking collectives: 19.3 us -> none  [the longest x1 7.89 us: local(): keys_block = lax.all_gather(cache_keys, 'dp', axis=0, tiled=True)]
    dot_general x12 -> x8, matrix products: 51 us -> 43.5 us  [the longest x1 21.7 us: local(): jnp.dot(hidden, down_weight[0], preferred_element_type=jnp.float32) * share]
  transfers between devices with their start and end apart: 8 -> 0, of which waited for: 7 -> 0; matrix products, arithmetic and copies ran while one was open for 2% -> 0% of each run, Pallas kernels for 0% -> 0%
where the time goes in v1:
time: 250 us; the launch traced here: 248 us
  Pallas kernels  178 us (71%)
  matrix products  43.7 us (17%)
  other arithmetic  16.2 us (6%)
  local copies, waits for them, and re-layouts  10.1 us (4%)
    pallas_call x7, Pallas kernels, exchange(): pl.pallas_call(functools.partial(exchange_kernel, kinds, sizes), out_shap...  94.7 us
    pallas_call x1, Pallas kernels, spread(): pl.pallas_call(functools.partial(spread_kernel, sizes), out_shape=(jax.Sh...  41.8 us
    pallas_call x1, Pallas kernels, collect(): pl.pallas_call(functools.partial(collect_kernel, sizes), out_shape=jax.Sh...  41.5 us
    dot_general x1, matrix products, local(): jnp.dot(hidden, down_weight[0], preferred_element_type=jnp.float32) * share  21.7 us
    dot_general x1, matrix products, local(): lax.dot_general(rows, gate_weight[0], contract_last, preferred_element_ty...  12.3 us

profile of v1, /device:TPU:0, one launch (start us, length us, event | category | flops | bytes accessed | tf_op | source)
XLA Modules:
  0.0 248.4 jit_solution(12986474497009830734)
XLA Ops:
  0.0 1.3 fusion.39
  1.3 0.8 fusion.44
  2.1 1.3 convert_bitcast_fusion.refs_3_
  3.6 1.8 fusion.41.refs_0_
  5.4 19.3 %exchange_0.1 = (bf16[4,32,1024]{2,1,0:T(8,128)(2,1)}, bf16[2,512,256]{2,1,0:T(8,128)(2,1)}, bf16[2,512,256]{2,1,0:T(8,128)(2,1)}, f32[2,2,512]{2,1,0:T(2,128)}) custom-call(bf16[32,4096]{1,0:T(8,128)(2,1)} %fusion.41.refs_0_, bf16[512,256]{1,0:T(8,128)(2,1)} %refs_1_.1, bf16[512,256]{1,0:T(8,128)(2,1)} %refs_2_.1, f32[2,512]{1,0:T(2,128)} %convert_bitcast_fusion.refs_3_), custom_call_target="tpu_custom_call" | custom-call | tf_op jit(solution)/shard_map/exchange_0/pallas_call | solution.py:154
  24.7 1.2 concatenate.29
  25.9 0.9 copy.36
  28.2 1.2 fusion.52
  29.4 1.3 fusion.51
  30.6 2.0 fusion.50
  32.7 0.9 pad_maximum_fusion
  33.6 19.1 %exchange_1.1 = f32[4,32,1536]{2,1,0:T(8,128)} custom-call(f32[4,32,1536]{2,1,0:T(8,128)} %bitcast.80), custom_call_target="tpu_custom_call" | custom-call | tf_op jit(solution)/shard_map/exchange_1/pallas_call | solution.py:154
  52.7 1.2 reduce_sum.64
  55.6 12.8 %exchange_2.1 = (bf16[2,32,1024]{2,1,0:T(8,128)(2,1)}, bf16[8,32,512]{2,1,0:T(8,128)(2,1)}) custom-call(bf16[32,1024]{1,0:T(8,128)(2,1)} %bitcast.91, bf16[32,512]{1,0:T(8,128)(2,1)} %pad_maximum_fusion.1.refs_1_), custom_call_target="tpu_custom_call" | custom-call | tf_op jit(solution)/shard_map/exchange_2/pallas_call | solution.py:154
  68.4 1.0 fusion.48
  69.8 1.0 reshape.151
  71.0 1.6 fusion.49
  74.6 11.4 %exchange_3.1 = bf16[4,64,1024]{2,1,0:T(8,128)(2,1)} custom-call(bf16[64,1024]{1,0:T(8,128)(2,1)} %convert_element_type.48.refs_0_), custom_call_target="tpu_custom_call" | custom-call | tf_op jit(solution)/shard_map/exchange_3/pallas_call | solution.py:154
  86.0 2.8 %fusion.20.refs_0_ = f32[4,4,16,1024]{3,2,1,0:T(8,128)} fusion(bf16[4,4,16,1024]{3,2,1,0:T(8,128)(2,1)} %bitcast.85, bf16[1024,1024]{1,0:T(8,128)(2,1)S(1)} %copy-done), kind=kOutput, calls=%fused_computation.15 | convolution fusion | flops 536870912 | bytes 3670016 | tf_op jit(solution)/shard_map/dot_general | solution.py:515
  88.8 13.7 %exchange_4.1 = f32[4,4,16,1024]{3,2,1,0:T(8,128)} custom-call(f32[4,4,16,1024]{3,2,1,0:T(8,128)} %fusion.20.refs_0_), custom_call_target="tpu_custom_call" | custom-call | tf_op jit(solution)/shard_map/exchange_4/pallas_call | solution.py:154
  102.5 2.0 reduce_sum.66.refs_0_
  104.5 10.7 %exchange_5.1 = f32[16,4096]{1,0:T(8,128)} custom-call(f32[4,16,1024]{2,1,0:T(8,128)} %reduce_sum.66.refs_0_), custom_call_target="tpu_custom_call" | custom-call | tf_op jit(solution)/shard_map/exchange_5/pallas_call | solution.py:154
  115.2 1.1 multiply_reduce_fusion
  116.3 1.0 multiply_convert_fusion.1.x_ref
  118.3 41.8 %spread.1 = (bf16[2,4,2,2,16,4096]{5,4,3,2,1,0:T(8,128)(2,1)}, f32[2,4,2,2,16,128]{5,4,3,2,1,0:T(8,128)}) custom-call(bf16[16,4096]{1,0:T(8,128)(2,1)} %copy-done.8, f32[16,128]{1,0:T(8,128)} %select_reduce_fusion.g_ref), custom_call_target="tpu_custom_call" | custom-call | tf_op jit(solution)/shard_map/spread/pallas_call | solution.py:280
  160.1 1.1 constant_dynamic-slice_fusion
  161.3 12.3 %fusion.4 = f32[512,1536]{1,0:T(8,128)} fusion(bf16[512,4096]{1,0:T(8,128)(2,1)} %bitcast.96, bf16[1,1536,4096]{2,1,0:T(8,128)(2,1)} %param.27), kind=kOutput, calls=%fused_computation.4 | convolution fusion | flops 6442450944 | bytes 19922944 | tf_op jit(solution)/shard_map/dot_general | solution.py:540
  173.7 21.7 %multiply_convert_fusion = bf16[512,4096]{1,0:T(8,128)(2,1)} fusion(bf16[1,1536,4096]{2,1,0:T(8,128)(2,1)} %param.29, f32[512]{0:T(512)S(1)} %bitcast.95, bf16[512,4096]{1,0:T(8,128)(2,1)} %bitcast.97, bf16[1,1536,4096]{2,1,0:T(8,128)(2,1)} %param.28, f32[512,1536]{1,0:T(8,128)} %fusion.4), kind=kOutput, calls=%fused_computation.6 | convolution fusion | flops 12893814784 | bytes 36702208 | tf_op jit(solution)/shard_map/dot_general | solution.py:546
  195.4 41.5 %collect.1 = f32[16,4096]{1,0:T(8,128)} custom-call(bf16[2,4,2,2,16,4096]{5,4,3,2,1,0:T(8,128)(2,1)} %bitcast.79), custom_call_target="tpu_custom_call" | custom-call | tf_op jit(solution)/shard_map/collect/pallas_call | solution.py:386
  236.9 1.6 add_convert_fusion.refs_0_
  238.6 7.9 %exchange_8.1 = bf16[4,16,4096]{2,1,0:T(8,128)(2,1)} custom-call(bf16[16,4096]{1,0:T(8,128)(2,1)} %add_convert_fusion.refs_0_), custom_call_target="tpu_custom_call" | custom-call | tf_op jit(solution)/shard_map/exchange_8/pallas_call | solution.py:154
  246.5 1.9 copy.61
  (58 shorter events, 7.0 us)
Async XLA Ops:
  0.0 86.0 %copy-start = (bf16[1024,1024]{1,0:T(8,128)(2,1)S(1)}, bf16[1024,1024]{1,0:T(8,128)(2,1)}, u32[]{:S(2)}) copy-start(bf16[1024,1024]{1,0:T(8,128)(2,1)} %param.20) | copy-start | bytes 6291460
  0.0 28.2 %copy-start.5 = (bf16[1024,256]{1,0:T(8,128)(2,1)S(1)}, bf16[1024,256]{1,0:T(8,128)(2,1)}, u32[]{:S(2)}) copy-start(bf16[1024,256]{1,0:T(8,128)(2,1)} %param.19) | copy-start | bytes 1572868
  24.7 4.7 %copy-start.3 = (bf16[4,32,1024]{2,1,0:T(8,128)(2,1)S(1)}, bf16[4,32,1024]{2,1,0:T(8,128)(2,1)}, u32[]{:S(2)}) copy-start(bf16[4,32,1024]{2,1,0:T(8,128)(2,1)} %get-tuple-element.14) | copy-start | bytes 786436
  33.6 37.2 %copy-start.7 = (bf16[2,512,256]{2,1,0:T(8,128)(2,1)S(1)}, bf16[2,512,256]{2,1,0:T(8,128)(2,1)}, u32[]{:S(2)}) copy-start(bf16[2,512,256]{2,1,0:T(8,128)(2,1)} %get-tuple-element.17) | copy-start | bytes 1572868
  71.0 2.2 copy-start.6
  86.0 29.2 %copy-start.4 = (bf16[64,4096]{1,0:T(8,128)(2,1)S(1)}, bf16[64,4096]{1,0:T(8,128)(2,1)}, u32[]{:S(2)}) copy-start(bf16[64,4096]{1,0:T(8,128)(2,1)} %param.15) | copy-start | bytes 1572868
  88.8 27.5 %copy-start.9 = (f32[4096]{0:T(1024)S(1)}, f32[4096]{0:T(1024)}, u32[]{:S(2)}) copy-start(f32[4096]{0:T(1024)} %param.24) | copy-start | bytes 49156
  88.8 28.5 %copy-start.10 = (bf16[4096,4]{0,1:T(4,128)(2,1)S(1)}, bf16[4096,4]{0,1:T(4,128)(2,1)}, u32[]{:S(2)}) copy-start(bf16[4096,4]{0,1:T(4,128)(2,1)} %param.25) | copy-start | bytes 98308
  117.4 0.9 copy-start.8
  195.4 41.5 %copy-start.2 = (f32[16,4096]{1,0:T(8,128)S(1)}, f32[16,4096]{1,0:T(8,128)}, u32[]{:S(2)}) copy-start(f32[16,4096]{1,0:T(8,128)} %exchange_5.1) | copy-start | bytes 786436
  195.4 53.0 %copy-start.1 = (bf16[1024,1024]{1,0:T(8,128)(2,1)S(1)}, bf16[1024,1024]{1,0:T(8,128)(2,1)}, u32[]{:S(2)}) copy-start(bf16[1024,1024]{1,0:T(8,128)(2,1)} %param.20) | copy-start | bytes 6291460

commit v2 on v1

--- a/solution.py
+++ b/solution.py
@@ -199,216 +199,345 @@
         return copy
 
 
-def spread_kernel(sizes, x_ref, g_ref, out, gates, send, recv, local):
+def flat_rows(block, rows):
+    if block.shape[-2] % 16 == 0:
+        return block.reshape(rows, block.shape[-1])
+    return block.astype(jnp.float32).reshape(rows, block.shape[-1]).astype(block.dtype)
+
+
+def open_rows(block, lead):
+    if lead[-1] % 16 == 0:
+        return block.astype(jnp.bfloat16).reshape(lead + block.shape[-1:])
+    return block.reshape(lead + block.shape[-1:]).astype(jnp.bfloat16)
+
+
+def spread_kernel(
+    sizes, pieces, x_ref, g_ref, gate_ref, up_ref, hidden, gates,
+    rows, gate_w, up_w, gate_sum, up_sum, send, recv, local, weight_sems,
+):
     dps, fs, levels = sizes["dp"], sizes["fsdp"], sizes["expert"] // 2
+    place = (
+        lax.axis_index("dp"),
+        lax.axis_index("fsdp"),
+        lax.axis_index("expert") // 2,
+        lax.rem(lax.axis_index("expert"), 2),
+    )
     own = [
-        pltpu.make_async_copy(
-            x_ref,
-            out.at[
-                lax.axis_index("dp"),
-                lax.axis_index("fsdp"),
-                lax.axis_index("expert") // 2,
-                lax.rem(lax.axis_index("expert"), 2),
-            ],
-            local.at[0],
-        ),
-        pltpu.make_async_copy(
-            g_ref,
-            gates.at[
-                lax.axis_index("dp"),
-                lax.axis_index("fsdp"),
-                lax.axis_index("expert") // 2,
-                lax.rem(lax.axis_index("expert"), 2),
-            ],
-            local.at[1],
-        ),
+        pltpu.make_async_copy(x_ref, rows.at[place], local.at[0]),
+        pltpu.make_async_copy(g_ref, gates.at[place], local.at[1]),
     ]
     for copy in own:
         copy.start()
+    wide = x_ref.shape[-1] // pieces
+    half = wide // 2
+    loads = []
+    for j in range(pieces):
+        cols = pl.ds(j * wide, wide)
+        pair = [
+            pltpu.make_async_copy(gate_ref.at[0, :, cols], gate_w.at[:, cols], weight_sems.at[2 * j]),
+            pltpu.make_async_copy(up_ref.at[0, :, cols], up_w.at[:, cols], weight_sems.at[2 * j + 1]),
+        ]
+        loads.append(pair)
     d, f, e, y, c = greet(sizes)
-    half = x_ref.shape[-1] // 2
-    low, high = pl.ds(0, half), pl.ds(half, half)
     go = Sender(send, recv)
-    copies = []
-    for k in range(1, fs):
-        to = {"fsdp": lax.rem(f + k, fs)}
-        copies.append(go(x_ref, out.at[d, f, y, c], to))
-        copies.append(go(g_ref, gates.at[d, f, y, c], to))
+    flying = {}
+
+    def start(phase, j):
+        low, high = pl.ds(j * wide, half), pl.ds(j * wide + half, half)
+        full = pl.ds(j * wide, wide)
+        copies = []
+        if phase == 0:
+            for k in range(1, fs):
+                to = {"fsdp": lax.rem(f + k, fs)}
+                copies.append(go(x_ref.at[:, full], rows.at[d, f, y, c, :, full], to))
+                if j == 0:
+                    copies.append(go(g_ref, gates.at[d, f, y, c], to))
+        elif phase == 1:
+            for k in range(1, dps):
+                to = {"dp": lax.rem(d + k, dps)}
+                block = rows.at[d, :, y, c, :, low]
+                copies.append(go(block, block, to))
+                if j == 0:
+                    block = gates.at[d, :, y, c]
+                    copies.append(go(block, block, to))
+            for k in range(1, levels):
+                to = {"expert": lax.rem(y + k, levels) * 2 + c}
+                block = rows.at[d, :, y, c, :, high]
+                copies.append(go(block, block, to))
+        elif phase == 2:
+            for k in range(1, levels):
+                to = {"expert": lax.rem(y + k, levels) * 2 + c}
+                block = rows.at[:, :, y, c, :, low]
+                copies.append(go(block, block, to))
+                if j == 0:
+                    block = gates.at[:, :, y, c]
+                    copies.append(go(block, block, to))
+            for k in range(1, dps):
+                to = {"dp": lax.rem(d + k, dps)}
+                block = rows.at[d, :, :, c, :, high]
+                copies.append(go(block, block, to))
+        else:
+            to = {"expert": y * 2 + 1 - c}
+            block = rows.at[:, :, :, c, :, full]
+            copies.append(go(block, block, to))
+            if j == 0:
+                block = gates.at[:, :, :, c]
+                copies.append(go(block, block, to))
+        flying[phase, j] = copies
+
+    def finish(phase, j):
+        for copy in flying.pop((phase, j)):
+            copy.wait()
+
+    for j in range(pieces):
+        start(0, j)
+    for pair in loads:
+        for copy in pair:
+            copy.start()
     for copy in own:
         copy.wait()
-    for copy in copies:
-        copy.wait()
-    copies = []
-    for k in range(1, dps):
-        to = {"dp": lax.rem(d + k, dps)}
-        part = out.at[d, :, y, c, :, low]
-        copies.append(go(part, part, to))
-        part = gates.at[d, :, y, c]
-        copies.append(go(part, part, to))
-    for k in range(1, levels):
-        to = {"expert": lax.rem(y + k, levels) * 2 + c}
-        part = out.at[d, :, y, c, :, high]
-        copies.append(go(part, part, to))
-    for copy in copies:
-        copy.wait()
-    copies = []
-    for k in range(1, levels):
-        to = {"expert": lax.rem(y + k, levels) * 2 + c}
-        part = out.at[:, :, y, c, :, low]
-        copies.append(go(part, part, to))
-        part = gates.at[:, :, y, c]
-        copies.append(go(part, part, to))
-    for k in range(1, dps):
-        to = {"dp": lax.rem(d + k, dps)}
-        part = out.at[d, :, :, c, :, high]
-        copies.append(go(part, part, to))
-    for copy in copies:
-        copy.wait()
-    to = {"expert": y * 2 + 1 - c}
-    part = out.at[:, :, :, c]
-    copies = [go(part, part, to)]
-    part = gates.at[:, :, :, c]
-    copies.append(go(part, part, to))
-    for copy in copies:
-        copy.wait()
-
-
-def spread(sizes, number, rows, shares):
+    every, units = hidden.shape
+    tile = 256 if units % 256 == 0 else 128
+    for step in range(pieces + 3):
+        for phase in (3, 2, 1):
+            j = step - phase + 1
+            if 0 <= j < pieces:
+                finish(phase - 1, j)
+                start(phase, j)
+        j = step - 3
+        if j < 0:
+            continue
+        finish(3, j)
+        for copy in loads[j]:
+            copy.wait()
+
+        @pl.loop(0, units // tile)
+        def _(i, j=j):
+            full = pl.ds(j * wide, wide)
+            picked = pl.ds(pl.multiple_of(i * tile, tile), tile)
+            block = flat_rows(rows[:, :, :, :, :, full], every)
+            last = (((1,), (1,)), ((), ()))
+            g = lax.dot_general(
+                block, gate_w[picked, full], last, preferred_element_type=jnp.float32
+            )
+            u = lax.dot_general(block, up_w[picked, full], last, preferred_element_type=jnp.float32)
+            if j > 0:
+                g += gate_sum[:, picked]
+                u += up_sum[:, picked]
+            if j < pieces - 1:
+                gate_sum[:, picked] = g
+                up_sum[:, picked] = u
+            else:
+                hidden[:, picked] = (g / (1.0 + jnp.exp(-g)) * u).astype(hidden.dtype)
+
+
+def spread(sizes, number, rows, shares, gate_weight, up_weight, pieces=4):
     dps, fs, levels = sizes["dp"], sizes["fsdp"], sizes["expert"] // 2
     lead = (dps, fs, levels, 2)
-    sems = 2 * (fs - 1) + 3 * (dps - 1) + 3 * (levels - 1) + 2
+    sub, width = rows.shape
+    every = dps * fs * levels * 2 * sub
+    units = gate_weight.shape[1]
+    gate_copies = (fs - 1) + (dps - 1) + (levels - 1) + 1
+    sems = pieces * ((fs - 1) + 2 * (dps - 1) + 2 * (levels - 1) + 1) + gate_copies
     return pl.pallas_call(
-        functools.partial(spread_kernel, sizes),
+        functools.partial(spread_kernel, sizes, pieces),
         out_shape=(
-            jax.ShapeDtypeStruct(lead + rows.shape, rows.dtype),
+            jax.ShapeDtypeStruct((every, units), jnp.bfloat16),
             jax.ShapeDtypeStruct(lead + shares.shape, shares.dtype),
         ),
-        in_specs=[pl.BlockSpec(memory_space=pl.ANY)] * 2,
-        out_specs=(pl.BlockSpec(memory_space=pl.ANY),) * 2,
+        in_specs=[pl.BlockSpec(memory_space=pl.ANY)] * 4,
+        out_specs=(pl.BlockSpec(memory_space=pltpu.VMEM), pl.BlockSpec(memory_space=pl.ANY)),
         scratch_shapes=[
+            pltpu.VMEM(lead + rows.shape, rows.dtype),
+            pltpu.VMEM((units, width), rows.dtype),
+            pltpu.VMEM((units, width), rows.dtype),
+            pltpu.VMEM((every, units), jnp.float32),
+            pltpu.VMEM((every, units), jnp.float32),
             pltpu.SemaphoreType.DMA((sems,)),
             pltpu.SemaphoreType.DMA((sems,)),
             pltpu.SemaphoreType.DMA((2,)),
+            pltpu.SemaphoreType.DMA((2 * pieces,)),
         ],
-        compiler_params=pltpu.CompilerParams(collective_id=number, has_side_effects=True),
+        compiler_params=pltpu.CompilerParams(
+            collective_id=number, has_side_effects=True, vmem_limit_bytes=56 << 20
+        ),
         name="spread",
-    )(rows, shares)
+    )(rows, shares, gate_weight, up_weight)
 
 
 def collect_kernel(
-    sizes, x_ref, out, first, one, two_a, two_b, three, r1, r2a, r2b, r3a, r3b, r4, send, recv, local
+    sizes, pieces, hidden, share, down_ref, out,
+    terms, down_w, one, two_a, two_b, three, r1, r2a, r2b, r3a, r3b, r4, send, recv, weight_sems,
 ):
     dps, fs, levels = sizes["dp"], sizes["fsdp"], sizes["expert"] // 2
-    half = out.shape[-1] // 2
-    low, high = pl.ds(0, half), pl.ds(half, half)
-    own = pltpu.make_async_copy(
-        x_ref.at[:, :, :, lax.rem(lax.axis_index("expert"), 2)], first, local.at[0]
-    )
-    own.start()
+    sub, width = out.shape
+    wide = width // pieces
+    half = wide // 2
+    loads = []
+    for j in range(pieces):
+        cols = pl.ds(j * wide, wide)
+        copy = pltpu.make_async_copy(down_ref.at[0, :, cols], down_w.at[:, cols], weight_sems.at[j])
+        copy.start()
+        loads.append(copy)
     d, f, e, y, c = greet(sizes)
     go = Sender(send, recv)
-    copy = go(x_ref.at[:, :, :, 1 - c], r1, {"expert": y * 2 + 1 - c})
-    own.wait()
-    copy.wait()
-
-    @pl.loop(0, dps * fs * levels)
-    def _(i):
-        p, q, r = i // (fs * levels), lax.rem(i // levels, fs), lax.rem(i, levels)
-        one[p, q, r] = (
-            first[p, q, r].astype(jnp.float32) + r1[p, q, r].astype(jnp.float32)
-        ).astype(one.dtype)
-
-    copies = []
-    for k in range(1, dps):
-        to = lax.rem(d + k, dps)
-        copies.append(go(one.at[to, :, :, :, low], r2a.at[k - 1], {"dp": to}))
-    for k in range(1, levels):
-        to = lax.rem(y + k, levels)
-        copies.append(go(one.at[:, :, to, :, high], r2b.at[k - 1], {"expert": to * 2 + c}))
-    for copy in copies:
-        copy.wait()
-
-    @pl.loop(0, fs * levels)
-    def _(i):
-        q, r = i // levels, lax.rem(i, levels)
-        total = one[d, q, r, :, low].astype(jnp.float32)
-        for k in range(dps - 1):
-            total += r2a[k, q, r].astype(jnp.float32)
-        two_a[q, r] = total.astype(two_a.dtype)
-
-    @pl.loop(0, dps * fs)
-    def _(i):
-        p, q = i // fs, lax.rem(i, fs)
-        total = one[p, q, y, :, high].astype(jnp.float32)
-        for k in range(levels - 1):
-            total += r2b[k, p, q].astype(jnp.float32)
-        two_b[p, q] = total.astype(two_b.dtype)
-
-    copies = []
-    for k in range(1, levels):
-        to = lax.rem(y + k, levels)
-        copies.append(go(two_a.at[:, to], r3a.at[k - 1], {"expert": to * 2 + c}))
-    for k in range(1, dps):
-        to = lax.rem(d + k, dps)
-        copies.append(go(two_b.at[to], r3b.at[k - 1], {"dp": to}))
-    for copy in copies:
-        copy.wait()
-
-    @pl.loop(0, fs)
-    def _(q):
-        total = two_a[q, y].astype(jnp.float32)
-        for k in range(levels - 1):
-            total += r3a[k, q].astype(jnp.float32)
-        three[q, :, low] = total.astype(three.dtype)
-        total = two_b[d, q].astype(jnp.float32)
-        for k in range(dps - 1):
-            total += r3b[k, q].astype(jnp.float32)
-        three[q, :, high] = total.astype(three.dtype)
-
-    copies = []
-    for k in range(1, fs):
-        to = lax.rem(f + k, fs)
-        copies.append(go(three.at[to], r4.at[k - 1], {"fsdp": to}))
-    for copy in copies:
-        copy.wait()
-    total = three[f].astype(jnp.float32)
-    for k in range(fs - 1):
-        total += r4[k].astype(jnp.float32)
-    out[...] = total
-
-
-def collect(sizes, number, terms):
+    flying = {}
+    wider = jnp.float32
+    tile = 256
+
+    def finish(phase, j):
+        for copy in flying.pop((phase, j)):
+            copy.wait()
+
+    def make(j):
+        loads[j].wait()
+
+        @pl.loop(0, wide // tile)
+        def _(i):
+            picked = pl.ds(pl.multiple_of(j * wide + i * tile, tile), tile)
+            product = jnp.dot(hidden[...], down_w[:, picked], preferred_element_type=wider)
+            terms[:, :, :, :, :, picked] = open_rows(
+                product * share[...], (dps, fs, levels, 2, sub)
+            )
+
+        full = pl.ds(j * wide, wide)
+        flying[0, j] = [
+            go(terms.at[:, :, :, 1 - c, :, full], r1.at[:, :, :, :, full], {"expert": y * 2 + 1 - c})
+        ]
+
+    def after_chip(j):
+        finish(0, j)
+        low, high = pl.ds(j * wide, half), pl.ds(j * wide + half, half)
+        full = pl.ds(j * wide, wide)
+        narrow = pl.ds(j * half, half)
+
+        @pl.loop(0, dps * fs * levels)
+        def _(i):
+            p, q, r = i // (fs * levels), lax.rem(i // levels, fs), lax.rem(i, levels)
+            one[p, q, r, :, full] = (
+                terms[p, q, r, c, :, full].astype(wider) + r1[p, q, r, :, full].astype(wider)
+            ).astype(one.dtype)
+
+        copies = []
+        for k in range(1, dps):
+            to = lax.rem(d + k, dps)
+            copies.append(
+                go(one.at[to, :, :, :, low], r2a.at[k - 1, :, :, :, narrow], {"dp": to})
+            )
+        for k in range(1, levels):
+            to = lax.rem(y + k, levels)
+            copies.append(
+                go(one.at[:, :, to, :, high], r2b.at[k - 1, :, :, :, narrow], {"expert": to * 2 + c})
+            )
+        flying[1, j] = copies
+
+    def after_first(j):
+        finish(1, j)
+        low, high = pl.ds(j * wide, half), pl.ds(j * wide + half, half)
+        narrow = pl.ds(j * half, half)
+
+        @pl.loop(0, fs * levels)
+        def _(i):
+            q, r = i // levels, lax.rem(i, levels)
+            total = one[d, q, r, :, low].astype(wider)
+            for k in range(dps - 1):
+                total += r2a[k, q, r, :, narrow].astype(wider)
+            two_a[q, r, :, narrow] = total.astype(two_a.dtype)
+
+        @pl.loop(0, dps * fs)
+        def _(i):
+            p, q = i // fs, lax.rem(i, fs)
+            total = one[p, q, y, :, high].astype(wider)
+            for k in range(levels - 1):
+                total += r2b[k, p, q, :, narrow].astype(wider)
+            two_b[p, q, :, narrow] = total.astype(two_b.dtype)
+
+        copies = []
+        for k in range(1, levels):
+            to = lax.rem(y + k, levels)
+            copies.append(
+                go(two_a.at[:, to, :, narrow], r3a.at[k - 1, :, :, narrow], {"expert": to * 2 + c})
+            )
+        for k in range(1, dps):
+            to = lax.rem(d + k, dps)
+            copies.append(go(two_b.at[to, :, :, narrow], r3b.at[k - 1, :, :, narrow], {"dp": to}))
+        flying[2, j] = copies
+
+    def after_second(j):
+        finish(2, j)
+        low, high = pl.ds(j * wide, half), pl.ds(j * wide + half, half)
+        full = pl.ds(j * wide, wide)
+        narrow = pl.ds(j * half, half)
+
+        @pl.loop(0, fs)
+        def _(q):
+            total = two_a[q, y, :, narrow].astype(wider)
+            for k in range(levels - 1):
+                total += r3a[k, q, :, narrow].astype(wider)
+            three[q, :, low] = total.astype(three.dtype)
+            total = two_b[d, q, :, narrow].astype(wider)
+            for k in range(dps - 1):
+                total += r3b[k, q, :, narrow].astype(wider)
+            three[q, :, high] = total.astype(three.dtype)
+
+        copies = []
+        for k in range(1, fs):
+            to = lax.rem(f + k, fs)
+            copies.append(go(three.at[to, :, full], r4.at[k - 1, :, full], {"fsdp": to}))
+        flying[3, j] = copies
+
+    def after_third(j):
+        finish(3, j)
+        full = pl.ds(j * wide, wide)
+        total = three[f, :, full].astype(wider)
+        for k in range(fs - 1):
+            total += r4[k, :, full].astype(wider)
+        out[:, full] = total
+
+    stages = (make, after_chip, after_first, after_second, after_third)
+    for step in range(pieces + len(stages) - 1):
+        for age, stage in enumerate(stages):
+            if 0 <= step - age < pieces:
+                stage(step - age)
+
+
+def collect(sizes, number, hidden, share, down_weight, sub, pieces=4):
     dps, fs, levels = sizes["dp"], sizes["fsdp"], sizes["expert"] // 2
-    rows, width = terms.shape[-2:]
+    units, width = down_weight.shape[1:]
     half = width // 2
-    kind = terms.dtype
-    sems = 1 + 2 * (dps - 1) + 2 * (levels - 1) + (fs - 1)
+    kind = jnp.bfloat16
+    sems = pieces * (1 + 2 * (dps - 1) + 2 * (levels - 1) + (fs - 1))
     return pl.pallas_call(
-        functools.partial(collect_kernel, sizes),
-        out_shape=jax.ShapeDtypeStruct((rows, width), jnp.float32),
-        in_specs=[pl.BlockSpec(memory_space=pl.ANY)],
+        functools.partial(collect_kernel, sizes, pieces),
+        out_shape=jax.ShapeDtypeStruct((sub, width), jnp.float32),
+        in_specs=[
+            pl.BlockSpec(memory_space=pltpu.VMEM),
+            pl.BlockSpec(memory_space=pltpu.VMEM),
+            pl.BlockSpec(memory_space=pl.ANY),
+        ],
         out_specs=pl.BlockSpec(memory_space=pltpu.VMEM),
         scratch_shapes=[
-            pltpu.VMEM((dps, fs, levels, rows, width), kind),
-            pltpu.VMEM((dps, fs, levels, rows, width), kind),
-            pltpu.VMEM((fs, levels, rows, half), kind),
-            pltpu.VMEM((dps, fs, rows, half), kind),
-            pltpu.VMEM((fs, rows, width), kind),
-            pltpu.VMEM((dps, fs, levels, rows, width), kind),
-            pltpu.VMEM((dps - 1, fs, levels, rows, half), kind),
-            pltpu.VMEM((levels - 1, dps, fs, rows, half), kind),
-            pltpu.VMEM((levels - 1, fs, rows, half), kind),
-            pltpu.VMEM((dps - 1, fs, rows, half), kind),
-            pltpu.VMEM((fs - 1, rows, width), kind),
+            pltpu.VMEM((dps, fs, levels, 2, sub, width), kind),
+            pltpu.VMEM((units, width), kind),
+            pltpu.VMEM((dps, fs, levels, sub, width), kind),
+            pltpu.VMEM((fs, levels, sub, half), kind),
+            pltpu.VMEM((dps, fs, sub, half), kind),
+            pltpu.VMEM((fs, sub, width), kind),
+            pltpu.VMEM((dps, fs, levels, sub, width), kind),
+            pltpu.VMEM((dps - 1, fs, levels, sub, half), kind),
+            pltpu.VMEM((levels - 1, dps, fs, sub, half), kind),
+            pltpu.VMEM((levels - 1, fs, sub, half), kind),
+            pltpu.VMEM((dps - 1, fs, sub, half), kind),
+            pltpu.VMEM((fs - 1, sub, width), kind),
             pltpu.SemaphoreType.DMA((sems,)),
             pltpu.SemaphoreType.DMA((sems,)),
-            pltpu.SemaphoreType.DMA((1,)),
+            pltpu.SemaphoreType.DMA((pieces,)),
         ],
         compiler_params=pltpu.CompilerParams(
             collective_id=number, has_side_effects=True, vmem_limit_bytes=56 << 20
         ),
         name="collect",
-    )(terms)
+    )(hidden, share, down_weight)
 
 
 def local(
@@ -532,20 +661,9 @@
     lanes = picks[:, :, None] == jnp.arange(128, dtype=jnp.int32)[None, None, :]
     shares = jnp.sum(jnp.where(lanes, gate_shares[:, :, None], 0.0), axis=1)
 
-    rows, shares = spread(sizes, 6, normed_mix, shares)
-    every = dps * window_rows
-    rows = rows.reshape(every, width)
-    share = lax.dynamic_slice_in_dim(shares.reshape(every, 128), e, 1, 1)
-    contract_last = (((1,), (1,)), ((), ()))
-    gate_values = lax.dot_general(
-        rows, gate_weight[0], contract_last, preferred_element_type=jnp.float32
-    )
-    lifted = lax.dot_general(rows, up_weight[0], contract_last, preferred_element_type=jnp.float32)
-    hidden = (jax.nn.silu(gate_values) * lifted).astype(jnp.bfloat16)
-    terms = (
-        jnp.dot(hidden, down_weight[0], preferred_element_type=jnp.float32) * share
-    ).astype(jnp.bfloat16)
-    mixture = collect(sizes, 7, terms.reshape(dps, fs, es // 2, 2, sub, width))
+    hidden, shares = spread(sizes, 6, normed_mix, shares, gate_weight, up_weight)
+    share = lax.dynamic_slice_in_dim(shares.reshape(dps * window_rows, 128), e, 1, 1)
+    mixture = collect(sizes, 7, hidden, share, down_weight, sub)
     (whole,) = exchange(
         sizes, 8, ((residual + mixture).astype(jnp.bfloat16), "gather", ("expert",))
     )

time: 250 us -> 215 us (0.86)
  matrix products: 43.7 us -> 9.5 us
    dot_general x2 -> x0, matrix products: 34 us -> none  [the longest x1 21.7 us: local(): jnp.dot(hidden, down_weight[0], preferred_element_type=jnp.float32) * share]
where the time goes in v2:
time: 215 us; the launch traced here: 214 us
  Pallas kernels  178 us (83%)
  other arithmetic  15.6 us (7%)
  local copies, waits for them, and re-layouts  10.3 us (5%)
  matrix products  9.5 us (4%)
    pallas_call x7, Pallas kernels, exchange(): pl.pallas_call(functools.partial(exchange_kernel, kinds, sizes), out_shap...  94 us
    pallas_call x1, Pallas kernels, spread(): pl.pallas_call(functools.partial(spread_kernel, sizes, pieces), out_shape...  48 us
    pallas_call x1, Pallas kernels, collect(): pl.pallas_call(functools.partial(collect_kernel, sizes, pieces), out_shap...  35.8 us

profile of v2, /device:TPU:0, one launch (start us, length us, event | category | flops | bytes accessed | tf_op | source)
XLA Modules:
  0.0 213.6 jit_solution(3171556375345963716)
XLA Ops:
  0.0 1.3 fusion.22
  1.3 1.9 fusion.24.refs_0_
  3.1 1.3 convert_bitcast_fusion.refs_3_
  4.4 19.3 %exchange_0.1 = (bf16[4,32,1024]{2,1,0:T(8,128)(2,1)}, bf16[2,512,256]{2,1,0:T(8,128)(2,1)}, bf16[2,512,256]{2,1,0:T(8,128)(2,1)}, f32[2,2,512]{2,1,0:T(2,128)}) custom-call(bf16[32,4096]{1,0:T(8,128)(2,1)} %fusion.24.refs_0_, bf16[512,256]{1,0:T(8,128)(2,1)} %refs_1_.1, bf16[512,256]{1,0:T(8,128)(2,1)} %refs_2_.1, f32[2,512]{1,0:T(2,128)} %convert_bitcast_fusion.refs_3_), custom_call_target="tpu_custom_call" | custom-call | tf_op jit(solution)/shard_map/exchange_0/pallas_call | solution.py:154
  23.7 2.2 %fusion.32 = f32[128,1024]{1,0:T(8,128)S(1)} fusion(bf16[128,1024]{1,0:T(8,128)(2,1)} %bitcast.58, bf16[1024,1024]{1,0:T(8,128)(2,1)} %param.17), kind=kOutput, calls=%fused_computation.63 | convolution fusion | flops 268435456 | bytes 2883584 | tf_op jit(solution)/shard_map/dot_general | solution.py:589
  26.4 0.9 pad_maximum_fusion
  27.3 19.1 %exchange_1.1 = f32[4,32,1536]{2,1,0:T(8,128)} custom-call(f32[4,32,1536]{2,1,0:T(8,128)} %bitcast.57), custom_call_target="tpu_custom_call" | custom-call | tf_op jit(solution)/shard_map/exchange_1/pallas_call | solution.py:154
  46.4 1.3 reduce_sum.64
  48.2 0.6 pad_maximum_fusion.1.refs_1_
  48.9 0.6 copy.55
  49.6 12.8 %exchange_2.1 = (bf16[2,32,1024]{2,1,0:T(8,128)(2,1)}, bf16[8,32,512]{2,1,0:T(8,128)(2,1)}) custom-call(bf16[32,1024]{1,0:T(8,128)(2,1)} %bitcast.68, bf16[32,512]{1,0:T(8,128)(2,1)} %pad_maximum_fusion.1.refs_1_), custom_call_target="tpu_custom_call" | custom-call | tf_op jit(solution)/shard_map/exchange_2/pallas_call | solution.py:154
  62.3 1.0 fusion.30
  63.5 1.6 reshape.145
  65.3 0.7 pad_add_fusion
  66.2 1.7 fusion.31
  67.9 1.5 copy-done.2
  70.4 2.3 %fusion.15 = bf16[64,2,4,128]{3,0,2,1:T(8,128)(2,1)S(1)} fusion(f32[2,4,64,1280]{3,2,1,0:T(8,128)} %copy-done.2, f32[2,4,64]{2,1,0:T(4,128)S(1)} %get-tuple-element.27, bf16[256,2,128]{2,0,1:T(8,128)(2,1)S(1)} %copy.36, bf16[1024,2,128]{2,0,1:T(8,128)(2,1)S(1)} %copy.35, f32[64,2,4]{0,2,1:T(4,128)S(1)} %bitcast.71), kind=kOutput, calls=%fused_computation.12 | convolution fusion | flops 170524672 | bytes 3411968 | tf_op jit(solution)/shard_map/kgtn,nkd->tkgd/dot_general | solution.py:635
  72.8 0.7 convert_element_type.42.refs_0_
  73.6 11.4 %exchange_3.1 = bf16[4,64,1024]{2,1,0:T(8,128)(2,1)} custom-call(bf16[64,1024]{1,0:T(8,128)(2,1)} %convert_element_type.42.refs_0_), custom_call_target="tpu_custom_call" | custom-call | tf_op jit(solution)/shard_map/exchange_3/pallas_call | solution.py:154
  84.9 2.7 %fusion.4.refs_0_ = f32[4,4,16,1024]{3,2,1,0:T(8,128)} fusion(bf16[4,4,16,1024]{3,2,1,0:T(8,128)(2,1)} %bitcast.62, bf16[1024,1024]{1,0:T(8,128)(2,1)S(1)} %copy-done), kind=kOutput, calls=%fused_computation.6 | convolution fusion | flops 536870912 | bytes 3670016 | tf_op jit(solution)/shard_map/dot_general | solution.py:644
  87.7 13.7 %exchange_4.1 = f32[4,4,16,1024]{3,2,1,0:T(8,128)} custom-call(f32[4,4,16,1024]{3,2,1,0:T(8,128)} %fusion.4.refs_0_), custom_call_target="tpu_custom_call" | custom-call | tf_op jit(solution)/shard_map/exchange_4/pallas_call | solution.py:154
  101.4 2.0 reduce_sum.66.refs_0_
  103.4 10.7 %exchange_5.1 = f32[16,4096]{1,0:T(8,128)} custom-call(f32[4,16,1024]{2,1,0:T(8,128)} %reduce_sum.66.refs_0_), custom_call_target="tpu_custom_call" | custom-call | tf_op jit(solution)/shard_map/exchange_5/pallas_call | solution.py:154
  114.1 1.1 multiply_reduce_fusion
  115.2 1.0 multiply_convert_fusion.x_ref
  116.6 0.7 select_reduce_fusion.g_ref
  117.3 48.0 %spread.1 = (bf16[512,1536]{1,0:T(8,128)(2,1)}, f32[2,4,2,2,16,128]{5,4,3,2,1,0:T(8,128)}) custom-call(bf16[16,4096]{1,0:T(8,128)(2,1)} %copy-done.5, f32[16,128]{1,0:T(8,128)} %select_reduce_fusion.g_ref, bf16[1,1536,4096]{2,1,0:T(8,128)(2,1)} %gate_ref.1, bf16[1,1536,4096]{2,1,0:T(8,128)(2,1)} %up_ref.1), custom_call_target="tpu_custom_call" | custom-call | tf_op jit(solution)/shard_map/spread/pallas_call | solution.py:342
  165.3 1.8 constant_dynamic-slice_fusion.share
  167.1 35.8 %collect.1 = f32[16,4096]{1,0:T(8,128)} custom-call(bf16[512,1536]{1,0:T(8,128)(2,1)} %get-tuple-element.19.hidden, f32[512,1]{1,0:T(8,128)} %constant_dynamic-slice_fusion.share, bf16[1,1536,4096]{2,1,0:T(8,128)(2,1)} %down_ref.1), custom_call_target="tpu_custom_call" | custom-call | tf_op jit(solution)/shard_map/collect/pallas_call | solution.py:510
  202.9 1.6 add_convert_fusion.refs_0_
  204.6 7.2 %exchange_8.1 = bf16[4,16,4096]{2,1,0:T(8,128)(2,1)} custom-call(bf16[16,4096]{1,0:T(8,128)(2,1)} %add_convert_fusion.refs_0_), custom_call_target="tpu_custom_call" | custom-call | tf_op jit(solution)/shard_map/exchange_8/pallas_call | solution.py:154
  211.8 1.9 copy.58
  (61 shorter events, 3.0 us)
Async XLA Ops:
  0.0 84.9 %copy-start = (bf16[1024,1024]{1,0:T(8,128)(2,1)S(1)}, bf16[1024,1024]{1,0:T(8,128)(2,1)}, u32[]{:S(2)}) copy-start(bf16[1024,1024]{1,0:T(8,128)(2,1)} %param.20) | copy-start | bytes 6291460
  0.0 25.9 %copy-start.6 = (bf16[1024,256]{1,0:T(8,128)(2,1)S(1)}, bf16[1024,256]{1,0:T(8,128)(2,1)}, u32[]{:S(2)}) copy-start(bf16[1024,256]{1,0:T(8,128)(2,1)} %param.18) | copy-start | bytes 1572868
  1.3 24.9 %copy-start.7 = (bf16[1024,256]{1,0:T(8,128)(2,1)S(1)}, bf16[1024,256]{1,0:T(8,128)(2,1)}, u32[]{:S(2)}) copy-start(bf16[1024,256]{1,0:T(8,128)(2,1)} %param.19) | copy-start | bytes 1572868
  23.7 2.2 %copy-start.3 = (bf16[4,32,1024]{2,1,0:T(8,128)(2,1)S(1)}, bf16[4,32,1024]{2,1,0:T(8,128)(2,1)}, u32[]{:S(2)}) copy-start(bf16[4,32,1024]{2,1,0:T(8,128)(2,1)} %get-tuple-element.14) | copy-start | bytes 786436
  46.4 18.8 %copy-start.11 = (f32[2,2,512]{2,1,0:T(2,128)S(1)}, f32[2,2,512]{2,1,0:T(2,128)}, u32[]{:S(2)}) copy-start(f32[2,2,512]{2,1,0:T(2,128)} %get-tuple-element.16) | copy-start | bytes 24580
  46.4 19.6 %copy-start.9 = (bf16[2,512,256]{2,1,0:T(8,128)(2,1)S(1)}, bf16[2,512,256]{2,1,0:T(8,128)(2,1)}, u32[]{:S(2)}) copy-start(bf16[2,512,256]{2,1,0:T(8,128)(2,1)} %get-tuple-element.17) | copy-start | bytes 1572868
  66.2 4.0 %copy-start.8 = (bf16[2,512,256]{2,1,0:T(8,128)(2,1)S(1)}, bf16[2,512,256]{2,1,0:T(8,128)(2,1)}, u32[]{:S(2)}) copy-start(bf16[2,512,256]{2,1,0:T(8,128)(2,1)} %get-tuple-element.13) | copy-start | bytes 1572868
  67.9 1.5 copy-start.2
  87.7 26.4 %copy-start.4 = (bf16[64,4096]{1,0:T(8,128)(2,1)S(1)}, bf16[64,4096]{1,0:T(8,128)(2,1)}, u32[]{:S(2)}) copy-start(bf16[64,4096]{1,0:T(8,128)(2,1)} %param.15) | copy-start | bytes 1572868
  87.7 27.5 %copy-start.10 = (f32[4096]{0:T(1024)S(1)}, f32[4096]{0:T(1024)}, u32[]{:S(2)}) copy-start(f32[4096]{0:T(1024)} %param.24) | copy-start | bytes 49156
  87.7 28.6 %copy-start.13 = (bf16[4096,4]{0,1:T(4,128)(2,1)S(1)}, bf16[4096,4]{0,1:T(4,128)(2,1)}, u32[]{:S(2)}) copy-start(bf16[4096,4]{0,1:T(4,128)(2,1)} %param.25) | copy-start | bytes 98308
  87.7 28.8 %copy-start.12 = (s32[1,64,2]{1,2,0:T(2,128)S(1)}, s32[1,64,2]{1,2,0:T(2,128)}, u32[]{:S(2)}) copy-start(s32[1,64,2]{1,2,0:T(2,128)} %param.26) | copy-start | bytes 1540
  116.3 1.0 copy-start.5
  167.1 35.8 %copy-start.1 = (f32[16,4096]{1,0:T(8,128)S(1)}, f32[16,4096]{1,0:T(8,128)}, u32[]{:S(2)}) copy-start(f32[16,4096]{1,0:T(8,128)} %exchange_5.1) | copy-start | bytes 786436

commit v3 on v2

--- a/solution.py
+++ b/solution.py
@@ -197,6 +197,103 @@
         self.next += 1
         copy.start()
         return copy
+
+
+def project_kernel(
+    sizes, att_ref, w_ref, out, tokens, weight, part, one, two, r1, r2, r3, send, recv, local
+):
+    fs, levels = sizes["fsdp"], sizes["expert"] // 2
+    loads = [
+        pltpu.make_async_copy(w_ref, weight, local.at[0]),
+        pltpu.make_async_copy(att_ref, tokens.at[0], local.at[1]),
+    ]
+    for copy in loads:
+        copy.start()
+    d, f, e, y, c = greet(sizes)
+    go = Sender(send, recv)
+    width = w_ref.shape[1]
+    sub = out.shape[0]
+    gathers = [None]
+    for k in range(1, fs):
+        gathers.append(go(att_ref, tokens.at[k], {"fsdp": lax.rem(f + k, fs)}))
+    for copy in loads:
+        copy.wait()
+    flying = {}
+
+    def owner(k):
+        return lax.rem(f - k + fs, fs)
+
+    def finish(phase, k):
+        for copy in flying.pop((phase, k)):
+            copy.wait()
+
+    def make(k):
+        if k > 0:
+            gathers[k].wait()
+        product = jnp.dot(tokens[k], weight[...], preferred_element_type=jnp.float32)
+        part[k] = product.reshape(levels, 2, sub, width)
+        flying[0, k] = [go(part.at[k, :, 1 - c], r1.at[k], {"expert": y * 2 + 1 - c})]
+
+    def after_chip(k):
+        finish(0, k)
+        one[k] = part[k, :, c] + r1[k]
+        copies = []
+        for m in range(1, levels):
+            to = lax.rem(y + m, levels)
+            copies.append(go(one.at[k, to], r2.at[k, m - 1], {"expert": to * 2 + c}))
+        flying[1, k] = copies
+
+    def after_level(k):
+        finish(1, k)
+        total = one[k, y]
+        for m in range(levels - 1):
+            total += r2[k, m]
+        two[k] = total
+        flying[2, k] = []
+        if k > 0:
+            flying[2, k].append(go(two.at[k], r3.at[k - 1], {"fsdp": owner(k)}))
+
+    stages = (make, after_chip, after_level)
+    for step in range(fs + len(stages) - 1):
+        for age, stage in enumerate(stages):
+            if 0 <= step - age < fs:
+                stage(step - age)
+    for k in range(fs):
+        finish(2, k)
+        source = lax.rem(f + k, fs)
+        columns = pl.ds(pl.multiple_of(source * width, 128), width)
+        out[:, columns] = two[0] if k == 0 else r3[k - 1]
+
+
+def project(sizes, number, attended, out_weight, sub):
+    fs, levels = sizes["fsdp"], sizes["expert"] // 2
+    rows, inner = attended.shape
+    width = out_weight.shape[1]
+    wide = jnp.float32
+    sems = (fs - 1) + fs + fs * (levels - 1) + (fs - 1)
+    return pl.pallas_call(
+        functools.partial(project_kernel, sizes),
+        out_shape=jax.ShapeDtypeStruct((sub, fs * width), wide),
+        in_specs=[pl.BlockSpec(memory_space=pl.ANY)] * 2,
+        out_specs=pl.BlockSpec(memory_space=pltpu.VMEM),
+        scratch_shapes=[
+            pltpu.VMEM((fs, rows, inner), attended.dtype),
+            pltpu.VMEM((inner, width), out_weight.dtype),
+            pltpu.VMEM((fs, levels, 2, sub, width), wide),
+            pltpu.VMEM((fs, levels, sub, width), wide),
+            pltpu.VMEM((fs, sub, width), wide),
+            pltpu.VMEM((fs, levels, sub, width), wide),
+            pltpu.VMEM((fs, levels - 1, sub, width), wide),
+            pltpu.VMEM((fs - 1, sub, width), wide),
+            pltpu.SemaphoreType.DMA((sems,)),
+            pltpu.SemaphoreType.DMA((sems,)),
+            pltpu.SemaphoreType.DMA((2,)),
+        ],
+        compiler_params=pltpu.CompilerParams(
+            collective_id=number, has_side_effects=True, vmem_limit_bytes=32 << 20
+        ),
+        name="project",
+    )(attended, out_weight)
 
 
 def flat_rows(block, rows):
@@ -575,14 +672,7 @@
     own_rows = lax.dynamic_slice_in_dim(window, d * part, part, 0)
     normed = rms_norm(own_rows, attention_gain)
     flags = occluded.astype(jnp.float32).T
-    columns, keys_block, values_block, flags_block = exchange(
-        sizes,
-        0,
-        (normed, "columns", ("fsdp",)),
-        (cache_keys, "gather", ("dp",)),
-        (cache_values, "gather", ("dp",)),
-        (flags, "gather", ("dp",)),
-    )
+    (columns,) = exchange(sizes, 0, (normed, "columns", ("fsdp",)))
     columns = columns.reshape(fs * part, width // fs)
     sums = jnp.concatenate(
         [
@@ -591,7 +681,14 @@
         ],
         axis=1,
     )
-    (sums,) = exchange(sizes, 1, (sums.reshape(fs, part, -1), "rows", ("fsdp",)))
+    sums, keys_block, values_block, flags_block = exchange(
+        sizes,
+        1,
+        (sums.reshape(fs, part, -1), "rows", ("fsdp",)),
+        (cache_keys, "gather", ("dp",)),
+        (cache_values, "gather", ("dp",)),
+        (flags, "gather", ("dp",)),
+    )
     sums = jnp.sum(sums, axis=0)
     positions = prefix_rows + f * token_rows + d * part + jnp.arange(part, dtype=jnp.int32)
     rotated = rotate(
@@ -640,16 +737,7 @@
     ) / totals.transpose(2, 0, 1)[..., None]
     attended = heads.reshape(token_rows, query_width).astype(jnp.bfloat16)
 
-    (attended,) = exchange(sizes, 3, (attended, "gather", ("fsdp",)))
-    head_terms = jnp.dot(
-        attended.reshape(window_rows, query_width), out_weight, preferred_element_type=jnp.float32
-    )
-    (head_terms,) = exchange(
-        sizes, 4, (head_terms.reshape(fs, es, sub, -1), "second", ("expert",))
-    )
-    (projected,) = exchange(
-        sizes, 5, (jnp.sum(head_terms, axis=0), "rows_to_columns", ("fsdp",))
-    )
+    projected = project(sizes, 3, attended, out_weight, sub)
     residual = lax.dynamic_slice_in_dim(window, e * sub, sub, 0).astype(jnp.float32) + projected
     normed_mix = rms_norm(residual, feedforward_gain)
     logits = jnp.dot(normed_mix, router_weight, preferred_element_type=jnp.float32)

time: 215 us -> 190 us (0.88)
  Pallas kernels: 178 us -> 161 us
  other arithmetic: 15.6 us -> 10.3 us
  matrix products: 9.5 us -> 6.17 us
    pallas_call x7 -> x4, Pallas kernels: 94 us -> 51.6 us  [exchange(): pl.pallas_call(functools.partial(exchange_kernel, kinds, sizes), out_shap...]
    pallas_call x0 -> x1, Pallas kernels: none -> 27 us  [project(): pl.pallas_call(functools.partial(project_kernel, sizes), out_shape=jax.Sh...]
    dot_general x1 -> x0, matrix products: 2.74 us -> none  [local(): jnp.dot(attended.reshape(window_rows, query_width), out_weight, preferred...]
    unnamed x33 -> x35, local copies, waits for them, and re-layouts: 4.27 us -> 5.87 us
where the time goes in v3:
time: 190 us; the launch traced here: 189 us
  Pallas kernels  161 us (85%)
  local copies, waits for them, and re-layouts  11.4 us (6%)
  other arithmetic  10.3 us (5%)
  matrix products  6.17 us (3%)
    pallas_call x4, Pallas kernels, exchange(): pl.pallas_call(functools.partial(exchange_kernel, kinds, sizes), out_shap...  51.6 us
    pallas_call x1, Pallas kernels, spread(): pl.pallas_call(functools.partial(spread_kernel, sizes, pieces), out_shape...  46.2 us
    pallas_call x1, Pallas kernels, collect(): pl.pallas_call(functools.partial(collect_kernel, sizes, pieces), out_shap...  35.8 us
    pallas_call x1, Pallas kernels, project(): pl.pallas_call(functools.partial(project_kernel, sizes), out_shape=jax.Sh...  27 us
    unnamed x35, local copies, waits for them, and re-layouts  5.87 us

profile of v3, /device:TPU:0, one launch (start us, length us, event | category | flops | bytes accessed | tf_op | source)
XLA Modules:
  0.0 189.0 jit_solution(11633902229305424739)
XLA Ops:
  0.0 1.3 fusion.20
  1.3 1.8 fusion.22.refs_0_
  3.1 10.6 %exchange_0.1 = bf16[4,32,1024]{2,1,0:T(8,128)(2,1)} custom-call(bf16[32,4096]{1,0:T(8,128)(2,1)} %fusion.22.refs_0_), custom_call_target="tpu_custom_call" | custom-call | tf_op jit(solution)/shard_map/exchange_0/pallas_call | solution.py:154
  13.7 1.4 fusion.30
  15.2 0.2 fusion.31
  15.4 0.2 fusion.32
  15.7 0.9 pad_maximum_fusion
  16.6 0.6 convert_bitcast_fusion.refs_3_
  17.2 23.2 %exchange_1.1 = (f32[4,32,1536]{2,1,0:T(8,128)}, bf16[2,512,256]{2,1,0:T(8,128)(2,1)}, bf16[2,512,256]{2,1,0:T(8,128)(2,1)}, f32[2,2,512]{2,1,0:T(2,128)}) custom-call(f32[4,32,1536]{2,1,0:T(8,128)} %bitcast.53, bf16[512,256]{1,0:T(8,128)(2,1)} %refs_1_.1, bf16[512,256]{1,0:T(8,128)(2,1)} %refs_2_.1, f32[2,512]{1,0:T(2,128)} %convert_bitcast_fusion.refs_3_), custom_call_target="tpu_custom_call" | custom-call | tf_op jit(solution)/shard_map/exchange_1/pallas_call | solution.py:154
  40.5 1.2 reduce_sum.55
  42.0 0.2 add_convert_fusion.1
  42.3 0.6 pad_maximum_fusion.1.refs_1_
  43.0 0.6 copy.54
  43.6 9.9 %exchange_2.1 = (bf16[2,32,1024]{2,1,0:T(8,128)(2,1)}, bf16[8,32,512]{2,1,0:T(8,128)(2,1)}) custom-call(bf16[32,1024]{1,0:T(8,128)(2,1)} %bitcast.60, bf16[32,512]{1,0:T(8,128)(2,1)} %pad_maximum_fusion.1.refs_1_), custom_call_target="tpu_custom_call" | custom-call | tf_op jit(solution)/shard_map/exchange_2/pallas_call | solution.py:154
  53.6 1.0 fusion.28
  54.8 1.0 reshape.141
  55.9 0.9 copy.38
  57.0 1.8 fusion.29
  58.8 1.5 copy-done.3
  60.3 0.6 fusion.2
  61.3 2.4 %fusion.13 = bf16[64,2,4,128]{3,0,2,1:T(8,128)(2,1)S(1)} fusion(f32[2,4,64,1280]{3,2,1,0:T(8,128)} %copy-done.3, f32[2,4,64]{2,1,0:T(4,128)S(1)} %get-tuple-element.27, bf16[256,2,128]{2,0,1:T(8,128)(2,1)S(1)} %copy.36, bf16[1024,2,128]{2,0,1:T(8,128)(2,1)S(1)} %copy.35, f32[64,2,4]{0,2,1:T(4,128)S(1)} %bitcast.63), kind=kOutput, calls=%fused_computation.10 | convolution fusion | flops 170524672 | bytes 3411968 | tf_op jit(solution)/shard_map/kgtn,nkd->tkgd/dot_general | solution.py:732
  63.9 1.6 copy-done.1
  65.5 27.0 %project.1 = f32[16,4096]{1,0:T(8,128)S(1)} custom-call(bf16[64,1024]{1,0:T(8,128)(2,1)S(1)} %convert_element_type.42.att_ref, bf16[1024,1024]{1,0:T(8,128)(2,1)S(1)} %copy-done.1), custom_call_target="tpu_custom_call" | custom-call | tf_op jit(solution)/shard_map/project/pallas_call | solution.py:274
  92.5 0.2 multiply_reduce_fusion
  92.8 0.1 fusion.33
  93.1 0.7 select_reduce_fusion.g_ref
  93.8 46.2 %spread.1 = (bf16[512,1536]{1,0:T(8,128)(2,1)}, f32[2,4,2,2,16,128]{5,4,3,2,1,0:T(8,128)}) custom-call(bf16[16,4096]{1,0:T(8,128)(2,1)} %copy-done.5, f32[16,128]{1,0:T(8,128)} %select_reduce_fusion.g_ref, bf16[1,1536,4096]{2,1,0:T(8,128)(2,1)} %gate_ref.1, bf16[1,1536,4096]{2,1,0:T(8,128)(2,1)} %up_ref.1), custom_call_target="tpu_custom_call" | custom-call | tf_op jit(solution)/shard_map/spread/pallas_call | solution.py:439
  140.1 1.8 constant_dynamic-slice_fusion.share
  141.9 35.8 %collect.1 = f32[16,4096]{1,0:T(8,128)} custom-call(bf16[512,1536]{1,0:T(8,128)(2,1)} %get-tuple-element.19.hidden, f32[512,1]{1,0:T(8,128)} %constant_dynamic-slice_fusion.share, bf16[1,1536,4096]{2,1,0:T(8,128)(2,1)} %down_ref.1), custom_call_target="tpu_custom_call" | custom-call | tf_op jit(solution)/shard_map/collect/pallas_call | solution.py:607
  177.7 1.6 add_convert_fusion.refs_0_
  179.3 7.8 %exchange_8.1 = bf16[4,16,4096]{2,1,0:T(8,128)(2,1)} custom-call(bf16[16,4096]{1,0:T(8,128)(2,1)} %add_convert_fusion.refs_0_), custom_call_target="tpu_custom_call" | custom-call | tf_op jit(solution)/shard_map/exchange_8/pallas_call | solution.py:154
  187.2 1.9 copy.57
  (59 shorter events, 1.8 us)
Async XLA Ops:
  0.0 13.7 %copy-start = (bf16[1024,1024]{1,0:T(8,128)(2,1)S(1)}, bf16[1024,1024]{1,0:T(8,128)(2,1)}, u32[]{:S(2)}) copy-start(bf16[1024,1024]{1,0:T(8,128)(2,1)} %param.17) | copy-start | bytes 6291460
  0.0 15.2 %copy-start.6 = (bf16[1024,256]{1,0:T(8,128)(2,1)S(1)}, bf16[1024,256]{1,0:T(8,128)(2,1)}, u32[]{:S(2)}) copy-start(bf16[1024,256]{1,0:T(8,128)(2,1)} %param.18) | copy-start | bytes 1572868
  0.0 15.4 %copy-start.7 = (bf16[1024,256]{1,0:T(8,128)(2,1)S(1)}, bf16[1024,256]{1,0:T(8,128)(2,1)}, u32[]{:S(2)}) copy-start(bf16[1024,256]{1,0:T(8,128)(2,1)} %param.19) | copy-start | bytes 1572868
  13.7 1.5 copy-start.2
  13.7 2.9 %copy-start.11 = (s32[512,2]{0,1:T(2,128)S(1)}, s32[512,2]{0,1:T(2,128)}, u32[]{:S(2)}) copy-start(s32[512,2]{0,1:T(2,128)} %param.23) | copy-start | bytes 12292
  40.5 15.3 %copy-start.9 = (bf16[2,512,256]{2,1,0:T(8,128)(2,1)S(1)}, bf16[2,512,256]{2,1,0:T(8,128)(2,1)}, u32[]{:S(2)}) copy-start(bf16[2,512,256]{2,1,0:T(8,128)(2,1)} %get-tuple-element.17) | copy-start | bytes 1572868
  42.0 14.8 %copy-start.12 = (f32[2,2,512]{2,1,0:T(2,128)S(1)}, f32[2,2,512]{2,1,0:T(2,128)}, u32[]{:S(2)}) copy-start(f32[2,2,512]{2,1,0:T(2,128)} %get-tuple-element.16) | copy-start | bytes 24580
  57.0 4.1 %copy-start.8 = (bf16[2,512,256]{2,1,0:T(8,128)(2,1)S(1)}, bf16[2,512,256]{2,1,0:T(8,128)(2,1)}, u32[]{:S(2)}) copy-start(bf16[2,512,256]{2,1,0:T(8,128)(2,1)} %get-tuple-element.13) | copy-start | bytes 1572868
  58.8 1.5 copy-start.3
  61.3 31.2 %copy-start.4 = (bf16[64,4096]{1,0:T(8,128)(2,1)S(1)}, bf16[64,4096]{1,0:T(8,128)(2,1)}, u32[]{:S(2)}) copy-start(bf16[64,4096]{1,0:T(8,128)(2,1)} %param.15) | copy-start | bytes 1572868
  63.7 29.1 %copy-start.10 = (f32[4096]{0:T(1024)S(1)}, f32[4096]{0:T(1024)}, u32[]{:S(2)}) copy-start(f32[4096]{0:T(1024)} %param.24) | copy-start | bytes 49156
  63.7 29.2 %copy-start.14 = (bf16[4096,4]{0,1:T(4,128)(2,1)S(1)}, bf16[4096,4]{0,1:T(4,128)(2,1)}, u32[]{:S(2)}) copy-start(bf16[4096,4]{0,1:T(4,128)(2,1)} %param.25) | copy-start | bytes 98308
  63.7 29.3 %copy-start.13 = (s32[1,64,2]{1,2,0:T(2,128)S(1)}, s32[1,64,2]{1,2,0:T(2,128)}, u32[]{:S(2)}) copy-start(s32[1,64,2]{1,2,0:T(2,128)} %param.26) | copy-start | bytes 1540
  63.9 1.6 copy-start.1
  92.8 1.0 copy-start.5

commit v4 on v3

--- a/solution.py
+++ b/solution.py
@@ -463,11 +463,11 @@
 
 
 def collect_kernel(
-    sizes, pieces, hidden, share, down_ref, out,
-    terms, down_w, one, two_a, two_b, three, r1, r2a, r2b, r3a, r3b, r4, send, recv, weight_sems,
+    sizes, pieces, hidden, share, residual, down_ref, out,
+    final, terms, down_w, one, two_a, two_b, three, r1, r2a, r2b, r3a, r3b, r4, send, recv, weight_sems,
 ):
     dps, fs, levels = sizes["dp"], sizes["fsdp"], sizes["expert"] // 2
-    sub, width = out.shape
+    sub, width = residual.shape
     wide = width // pieces
     half = wide // 2
     loads = []
@@ -589,31 +589,49 @@
         total = three[f, :, full].astype(wider)
         for k in range(fs - 1):
             total += r4[k, :, full].astype(wider)
-        out[:, full] = total
-
-    stages = (make, after_chip, after_first, after_second, after_third)
+        final[y, c, :, full] = (residual[:, full] + total).astype(final.dtype)
+        block = final.at[y, c, :, full]
+        flying[4, j] = [
+            go(block, block, {"expert": lax.rem(y + k, levels) * 2 + c}) for k in range(1, levels)
+        ]
+
+    def after_sum(j):
+        finish(4, j)
+        block = final.at[:, c, :, pl.ds(j * wide, wide)]
+        flying[5, j] = [go(block, block, {"expert": y * 2 + 1 - c})]
+
+    def after_rows(j):
+        finish(5, j)
+
+    stages = (
+        make, after_chip, after_first, after_second, after_third, after_sum, after_rows,
+    )
     for step in range(pieces + len(stages) - 1):
         for age, stage in enumerate(stages):
             if 0 <= step - age < pieces:
                 stage(step - age)
-
-
-def collect(sizes, number, hidden, share, down_weight, sub, pieces=4):
+    out[...] = final[...]
+
+
+def collect(sizes, number, hidden, share, residual, down_weight, pieces=4):
     dps, fs, levels = sizes["dp"], sizes["fsdp"], sizes["expert"] // 2
     units, width = down_weight.shape[1:]
+    sub = residual.shape[0]
     half = width // 2
     kind = jnp.bfloat16
-    sems = pieces * (1 + 2 * (dps - 1) + 2 * (levels - 1) + (fs - 1))
+    sems = pieces * (2 + 2 * (dps - 1) + 3 * (levels - 1) + (fs - 1))
     return pl.pallas_call(
         functools.partial(collect_kernel, sizes, pieces),
-        out_shape=jax.ShapeDtypeStruct((sub, width), jnp.float32),
+        out_shape=jax.ShapeDtypeStruct((levels, 2, sub, width), kind),
         in_specs=[
+            pl.BlockSpec(memory_space=pltpu.VMEM),
             pl.BlockSpec(memory_space=pltpu.VMEM),
             pl.BlockSpec(memory_space=pltpu.VMEM),
             pl.BlockSpec(memory_space=pl.ANY),
         ],
         out_specs=pl.BlockSpec(memory_space=pltpu.VMEM),
         scratch_shapes=[
+            pltpu.VMEM((levels, 2, sub, width), kind),
             pltpu.VMEM((dps, fs, levels, 2, sub, width), kind),
             pltpu.VMEM((units, width), kind),
             pltpu.VMEM((dps, fs, levels, sub, width), kind),
@@ -634,7 +652,7 @@
             collective_id=number, has_side_effects=True, vmem_limit_bytes=56 << 20
         ),
         name="collect",
-    )(hidden, share, down_weight)
+    )(hidden, share, residual, down_weight)
 
 
 def local(
@@ -672,7 +690,9 @@
     own_rows = lax.dynamic_slice_in_dim(window, d * part, part, 0)
     normed = rms_norm(own_rows, attention_gain)
     flags = occluded.astype(jnp.float32).T
-    (columns,) = exchange(sizes, 0, (normed, "columns", ("fsdp",)))
+    columns, keys_block = exchange(
+        sizes, 0, (normed, "columns", ("fsdp",)), (cache_keys, "gather", ("dp",))
+    )
     columns = columns.reshape(fs * part, width // fs)
     sums = jnp.concatenate(
         [
@@ -681,11 +701,10 @@
         ],
         axis=1,
     )
-    sums, keys_block, values_block, flags_block = exchange(
+    sums, values_block, flags_block = exchange(
         sizes,
         1,
         (sums.reshape(fs, part, -1), "rows", ("fsdp",)),
-        (cache_keys, "gather", ("dp",)),
         (cache_values, "gather", ("dp",)),
         (flags, "gather", ("dp",)),
     )
@@ -751,10 +770,7 @@
 
     hidden, shares = spread(sizes, 6, normed_mix, shares, gate_weight, up_weight)
     share = lax.dynamic_slice_in_dim(shares.reshape(dps * window_rows, 128), e, 1, 1)
-    mixture = collect(sizes, 7, hidden, share, down_weight, sub)
-    (whole,) = exchange(
-        sizes, 8, ((residual + mixture).astype(jnp.bfloat16), "gather", ("expert",))
-    )
+    whole = collect(sizes, 7, hidden, share, residual, down_weight)
     return whole.reshape(1, token_rows, width)
 
 

time: 190 us -> 184 us (0.968)
  Pallas kernels: 161 us -> 157 us
    pallas_call x4 -> x3, Pallas kernels: 51.6 us -> 43.1 us  [exchange(): pl.pallas_call(functools.partial(exchange_kernel, kinds, sizes), out_shap...]
    pallas_call x1, Pallas kernels: 35.8 us -> 40.4 us  [collect(): pl.pallas_call(functools.partial(collect_kernel, sizes, pieces), out_shap...]
where the time goes in v4:
time: 184 us
  Pallas kernels  157 us (85%)
  local copies, waits for them, and re-layouts  10.6 us (6%)
  other arithmetic  10.2 us (6%)
  matrix products  5.97 us (3%)
    pallas_call x1, Pallas kernels, spread(): pl.pallas_call(functools.partial(spread_kernel, sizes, pieces), out_shape...  46.2 us
    pallas_call x3, Pallas kernels, exchange(): pl.pallas_call(functools.partial(exchange_kernel, kinds, sizes), out_shap...  43.1 us
    pallas_call x1, Pallas kernels, collect(): pl.pallas_call(functools.partial(collect_kernel, sizes, pieces), out_shap...  40.4 us
    pallas_call x1, Pallas kernels, project(): pl.pallas_call(functools.partial(project_kernel, sizes), out_shape=jax.Sh...  27 us
    unnamed x35, local copies, waits for them, and re-layouts  5.88 us

profile of v4, /device:TPU:0, one launch (start us, length us, event | category | flops | bytes accessed | tf_op | source)
XLA Modules:
  0.0 184.1 jit_solution(14250337575250824726)
XLA Ops:
  0.0 1.3 fusion.20
  1.3 1.8 fusion.22.refs_0_
  3.1 13.0 %exchange_0.1 = (bf16[4,32,1024]{2,1,0:T(8,128)(2,1)}, bf16[2,512,256]{2,1,0:T(8,128)(2,1)}) custom-call(bf16[32,4096]{1,0:T(8,128)(2,1)} %fusion.22.refs_0_, bf16[512,256]{1,0:T(8,128)(2,1)} %refs_1_.2), custom_call_target="tpu_custom_call" | custom-call | tf_op jit(solution)/shard_map/exchange_0/pallas_call | solution.py:154
  16.1 1.4 fusion.30
  17.6 0.2 fusion.31
  17.8 0.2 fusion.32
  18.1 1.0 pad_maximum_fusion
  19.0 0.6 convert_bitcast_fusion.refs_2_
  19.6 18.4 %exchange_1.1 = (f32[4,32,1536]{2,1,0:T(8,128)}, bf16[2,512,256]{2,1,0:T(8,128)(2,1)}, f32[2,2,512]{2,1,0:T(2,128)}) custom-call(f32[4,32,1536]{2,1,0:T(8,128)} %bitcast.50, bf16[512,256]{1,0:T(8,128)(2,1)} %refs_1_.3, f32[2,512]{1,0:T(2,128)} %convert_bitcast_fusion.refs_2_), custom_call_target="tpu_custom_call" | custom-call | tf_op jit(solution)/shard_map/exchange_1/pallas_call | solution.py:154
  38.0 1.3 reduce_sum.55
  39.4 0.1 multiply_cosine_fusion
  39.5 0.2 add_convert_fusion
  39.8 0.6 pad_maximum_fusion.1.refs_1_
  40.5 0.6 copy.54
  41.2 11.8 %exchange_2.1 = (bf16[2,32,1024]{2,1,0:T(8,128)(2,1)}, bf16[8,32,512]{2,1,0:T(8,128)(2,1)}) custom-call(bf16[32,1024]{1,0:T(8,128)(2,1)} %bitcast.60, bf16[32,512]{1,0:T(8,128)(2,1)} %pad_maximum_fusion.1.refs_1_), custom_call_target="tpu_custom_call" | custom-call | tf_op jit(solution)/shard_map/exchange_2/pallas_call | solution.py:154
  52.9 1.0 fusion.28
  54.2 1.0 reshape.141
  55.3 0.7 pad_add_fusion
  56.2 1.6 fusion.29
  57.8 1.5 copy-done.2
  59.4 0.6 fusion.2
  60.2 0.1 concatenate.30
  60.4 2.3 %fusion.13 = bf16[64,2,4,128]{3,0,2,1:T(8,128)(2,1)S(1)} fusion(f32[2,4,64,1280]{3,2,1,0:T(8,128)} %copy-done.2, f32[2,4,64]{2,1,0:T(4,128)S(1)} %get-tuple-element.31, bf16[256,2,128]{2,0,1:T(8,128)(2,1)S(1)} %copy.36, bf16[1024,2,128]{2,0,1:T(8,128)(2,1)S(1)} %copy.35, f32[64,2,4]{0,2,1:T(4,128)S(1)} %bitcast.63), kind=kOutput, calls=%fused_computation.10 | convolution fusion | flops 170524672 | bytes 3411968 | tf_op jit(solution)/shard_map/kgtn,nkd->tkgd/dot_general | solution.py:751
  62.9 1.6 copy-done.1
  64.5 27.0 %project.1 = f32[16,4096]{1,0:T(8,128)S(1)} custom-call(bf16[64,1024]{1,0:T(8,128)(2,1)S(1)} %convert_element_type.39.att_ref, bf16[1024,1024]{1,0:T(8,128)(2,1)S(1)} %copy-done.1), custom_call_target="tpu_custom_call" | custom-call | tf_op jit(solution)/shard_map/project/pallas_call | solution.py:274
  91.5 1.1 multiply_reduce_fusion
  92.7 0.1 fusion.33
  93.0 0.7 select_reduce_fusion.g_ref
  93.7 46.2 %spread.1 = (bf16[512,1536]{1,0:T(8,128)(2,1)}, f32[2,4,2,2,16,128]{5,4,3,2,1,0:T(8,128)}) custom-call(bf16[16,4096]{1,0:T(8,128)(2,1)} %copy-done.5, f32[16,128]{1,0:T(8,128)} %select_reduce_fusion.g_ref, bf16[1,1536,4096]{2,1,0:T(8,128)(2,1)} %gate_ref.1, bf16[1,1536,4096]{2,1,0:T(8,128)(2,1)} %up_ref.1), custom_call_target="tpu_custom_call" | custom-call | tf_op jit(solution)/shard_map/spread/pallas_call | solution.py:439
  140.0 1.8 constant_dynamic-slice_fusion.share
  141.8 40.4 %collect.1 = bf16[2,2,16,4096]{3,2,1,0:T(8,128)(2,1)} custom-call(bf16[512,1536]{1,0:T(8,128)(2,1)} %get-tuple-element.21.hidden, f32[512,1]{1,0:T(8,128)} %constant_dynamic-slice_fusion.share, f32[16,4096]{1,0:T(8,128)} %copy-done.4, bf16[1,1536,4096]{2,1,0:T(8,128)(2,1)} %down_ref.1), custom_call_target="tpu_custom_call" | custom-call | tf_op jit(solution)/shard_map/collect/pallas_call | solution.py:623
  182.2 1.9 %copy.57 = bf16[1,64,4096]{2,1,0:T(8,128)(2,1)} copy(bf16[1,64,4096]{2,1,0:T(8,128)(2,1)} %bitcast.54) | data formatting | bytes 1048576
  (57 shorter events, 1.6 us)
Async XLA Ops:
  0.0 16.1 %copy-start = (bf16[1024,1024]{1,0:T(8,128)(2,1)S(1)}, bf16[1024,1024]{1,0:T(8,128)(2,1)}, u32[]{:S(2)}) copy-start(bf16[1024,1024]{1,0:T(8,128)(2,1)} %param.17) | copy-start | bytes 6291460
  0.0 17.5 %copy-start.6 = (bf16[1024,256]{1,0:T(8,128)(2,1)S(1)}, bf16[1024,256]{1,0:T(8,128)(2,1)}, u32[]{:S(2)}) copy-start(bf16[1024,256]{1,0:T(8,128)(2,1)} %param.18) | copy-start | bytes 1572868
  0.0 17.8 %copy-start.7 = (bf16[1024,256]{1,0:T(8,128)(2,1)S(1)}, bf16[1024,256]{1,0:T(8,128)(2,1)}, u32[]{:S(2)}) copy-start(bf16[1024,256]{1,0:T(8,128)(2,1)} %param.19) | copy-start | bytes 1572868
  16.1 1.5 copy-start.3
  16.1 2.9 %copy-start.11 = (s32[512,2]{0,1:T(2,128)S(1)}, s32[512,2]{0,1:T(2,128)}, u32[]{:S(2)}) copy-start(s32[512,2]{0,1:T(2,128)} %param.23) | copy-start | bytes 12292
  38.0 17.2 %copy-start.12 = (f32[2,2,512]{2,1,0:T(2,128)S(1)}, f32[2,2,512]{2,1,0:T(2,128)}, u32[]{:S(2)}) copy-start(f32[2,2,512]{2,1,0:T(2,128)} %get-tuple-element.18) | copy-start | bytes 24580
  38.0 18.0 %copy-start.9 = (bf16[2,512,256]{2,1,0:T(8,128)(2,1)S(1)}, bf16[2,512,256]{2,1,0:T(8,128)(2,1)}, u32[]{:S(2)}) copy-start(bf16[2,512,256]{2,1,0:T(8,128)(2,1)} %get-tuple-element.19) | copy-start | bytes 1572868
  56.2 4.0 %copy-start.8 = (bf16[2,512,256]{2,1,0:T(8,128)(2,1)S(1)}, bf16[2,512,256]{2,1,0:T(8,128)(2,1)}, u32[]{:S(2)}) copy-start(bf16[2,512,256]{2,1,0:T(8,128)(2,1)} %get-tuple-element.15) | copy-start | bytes 1572868
  57.8 1.5 copy-start.2
  62.7 29.9 %copy-start.10 = (f32[4096]{0:T(1024)S(1)}, f32[4096]{0:T(1024)}, u32[]{:S(2)}) copy-start(f32[4096]{0:T(1024)} %param.24) | copy-start | bytes 49156
  62.7 30.0 %copy-start.14 = (bf16[4096,4]{0,1:T(4,128)(2,1)S(1)}, bf16[4096,4]{0,1:T(4,128)(2,1)}, u32[]{:S(2)}) copy-start(bf16[4096,4]{0,1:T(4,128)(2,1)} %param.25) | copy-start | bytes 98308
  62.7 30.2 %copy-start.13 = (s32[1,64,2]{1,2,0:T(2,128)S(1)}, s32[1,64,2]{1,2,0:T(2,128)}, u32[]{:S(2)}) copy-start(s32[1,64,2]{1,2,0:T(2,128)} %param.26) | copy-start | bytes 1540
  62.9 1.6 copy-start.1
  92.6 47.4 %copy-start.4 = (f32[16,4096]{1,0:T(8,128)}, f32[16,4096]{1,0:T(8,128)S(1)}, u32[]{:S(2)}) copy-start(f32[16,4096]{1,0:T(8,128)S(1)} %get-tuple-element.24.residual) | copy-start | bytes 786436
  92.7 1.0 copy-start.5
